TPU v7x, 32 devices: a whole 2x2x4 slice. The times are simulated.
32 devices in a mesh: groups: 2 (over y), seq: 4 (over x, core), heads: 4 (over z).
Axes of the slice: x: 2, y: 2, z: 4, core: 2. Of those that a mesh axis runs over, the one named last changes fastest.
Arguments:
- tokens: bfloat16 [4096, 8192], P(('groups', 'seq'), 'heads'), parts along dimension 0, may hold values from -6 to 6
- xz_weight: bfloat16 [8192, 32768], P(None, ('heads', 'seq')), may hold values from -0.0625 to 0.0625
- bc_weight: bfloat16 [8192, 2048], P(None, 'heads'), may hold values from -0.0625 to 0.0625
- step_weight: bfloat16 [8192, 256], P(None, 'heads'), may hold values from -0.0625 to 0.0625
- step_bias: float32 [256], P('heads'), may hold values from -4 to -2
- decay_log: float32 [256], P('heads'), may hold values from -5.3 to -0.7
- skip_gain: float32 [256], P('heads'), may hold values from 0.5 to 2
- conv_weight: float32 [4, 16384], P(None, 'heads'), may hold values from -3 to 3
- conv_bias: float32 [16384], P('heads'), may hold values from -3 to 3
- bc_conv_weight: float32 [4, 2048], replicated, may hold values from -3 to 3
- bc_conv_bias: float32 [2048], replicated, may hold values from -3 to 3
- norm_gain: float32 [16384], P('heads'), may hold values from 0.1 to 1.9
- step_bounds: int32 [32], P('groups'), parts along dimension 0, may hold values from 0 to 2047, as said below
- readers: int32 [32], P('groups'), parts along dimension 0, may hold values from 0 to 3, as said below
Outputs:
- mixed: bfloat16 [4096, 16384], P(('groups', 'seq'), 'heads'), parts along dimension 0
- handoff: bfloat16 [8, 4, 256, 64, 128], P(('groups', 'heads'), None, 'seq'), parts along dimension 0
There are 2 independent parts, one for each index of `groups`. A program takes and returns all parts, laid end to end along the dimension named above; an argument that names none is the same for every part. Nothing has to cross between parts.
Inputs may be any that keep to these rules, and one draw needn't show every extreme that they name: `step_bounds`: boundary j * 4 + i, for i < 4, lies in section j: positions j * 512 to (j + 1) * 512 - 1. The first boundary is at position 0 and the last at 2047. `readers`: among the 4 boundaries of each section every reader appears exactly once.
All inputs are finite; a program needn't handle non-finite values.
Results may differ from a plain program's by a relative error of at most 0.0056.
Values may be sent and summed in bfloat16 or wider, within the bound.
A program may use at most 384 MiB of HBM per device.

v0:
```python
import jax
import jax.numpy as jnp
from jax import lax
from jax.sharding import PartitionSpec as P

H = 256
P_SIZE = 64
N = 128
G = 8
CH = 256


EPSILON = 1e-05
HIGHEST_PRECISION = lax.Precision.HIGHEST


def from_behind(value, axis, steps):
    count = lax.axis_size(axis)
    first, last = (max(0, -steps), min(count, count - steps))
    return lax.ppermute(value, axis, [(source, source + steps) for source in range(first, last)])


def entering(part, axis, combine, identity):
    place = lax.axis_index(axis)
    gathered = jax.tree.map(lambda a: lax.all_gather(a, axis), part)
    state = jax.tree.map(lambda a, e: jnp.zeros_like(a) + jnp.asarray(e, a.dtype), part, identity)

    def one(step, state):
        return combine(
            state, jax.tree.map(lambda a: lax.dynamic_index_in_dim(a, step, 0, False), gathered)
        )

    return lax.fori_loop(0, place, one, state)


def conv_rows(prefix, raw_rows, kernel, shift_bias):
    row_count = raw_rows.shape[0]
    padded = jnp.concatenate([prefix, raw_rows], axis=0).astype(jnp.float32)
    summed = jnp.broadcast_to(shift_bias[None, :], raw_rows.shape)
    for tap_index in range(kernel.shape[0]):
        summed = summed + kernel[tap_index][None, :] * padded[tap_index : tap_index + row_count]
    return jax.nn.silu(summed).astype(jnp.bfloat16)


def shards(
    tokens,
    xz_weight,
    bc_weight,
    step_weight,
    step_bias,
    decay_log,
    skip_gain,
    conv_weight,
    conv_bias,
    bc_conv_weight,
    bc_conv_bias,
    norm_gain,
    step_bounds,
    readers,
):
    head_devices = lax.axis_size("heads")
    section = lax.axis_index("seq")
    head_block = lax.axis_index("heads")
    local_heads = H // head_devices
    per_group = H // G
    local_groups = max(1, local_heads // per_group)
    group_heads = local_heads // local_groups
    first_group = head_block * local_heads // per_group
    gathered = lax.all_gather(tokens, "heads", axis=1, tiled=True)
    row_count = gathered.shape[0]
    xz_rows = jnp.dot(
        gathered,
        lax.all_gather(xz_weight, "seq", axis=1, tiled=True),
        preferred_element_type=jnp.float32,
    ).astype(jnp.bfloat16)
    head_cols = xz_rows.reshape(row_count, local_heads, 2 * P_SIZE)
    inner_raw = head_cols[:, :, :P_SIZE].reshape(row_count, local_heads * P_SIZE)
    gate_raw = head_cols[:, :, P_SIZE:].reshape(row_count, local_groups, group_heads, P_SIZE)
    bc_part = jnp.dot(gathered, bc_weight, preferred_element_type=jnp.float32).astype(jnp.bfloat16)
    step_raw = jnp.dot(gathered, step_weight, preferred_element_type=jnp.float32)
    bc_every = lax.all_gather(bc_part, "heads", axis=1, tiled=True)
    width_bc = local_groups * 2 * N
    bc_mine = lax.dynamic_slice_in_dim(bc_every, first_group * 2 * N, width_bc, 1)
    kernel_bc = lax.dynamic_slice_in_dim(bc_conv_weight, first_group * 2 * N, width_bc, 1)
    shift_bc = lax.dynamic_slice_in_dim(bc_conv_bias, first_group * 2 * N, width_bc, 0)
    taps = conv_weight.shape[0]
    joined = jnp.concatenate([inner_raw, bc_mine], axis=1)
    previous = from_behind(joined[row_count - taps + 1 :], "seq", 1)
    inner_conv = conv_rows(
        previous[:, : local_heads * P_SIZE], inner_raw, conv_weight, conv_bias
    ).reshape(row_count, local_groups, group_heads, P_SIZE)
    bc_conv = conv_rows(previous[:, local_heads * P_SIZE :], bc_mine, kernel_bc, shift_bc).reshape(
        row_count, local_groups, 2 * N
    )
    b_input = bc_conv[:, :, :N]
    c_input = bc_conv[:, :, N:]
    step_size = jax.nn.softplus(step_raw + step_bias[None, :]).reshape(
        row_count, local_groups, group_heads
    )
    decay_rate = -jnp.exp(decay_log).reshape(local_groups, group_heads)[None] * step_size
    blocks = row_count // CH
    causal = lax.broadcasted_iota(jnp.int32, (CH, CH), 0) >= lax.broadcasted_iota(
        jnp.int32, (CH, CH), 1
    )
    running = jnp.zeros((local_groups, group_heads, P_SIZE, N), jnp.float32)
    local_starts = []
    intra_parts = []
    cum_parts = []
    block_totals = []
    for block_index in range(blocks):
        first_row = block_index * CH
        inner_blk = inner_conv[first_row : first_row + CH]
        b_blk = b_input[first_row : first_row + CH]
        c_blk = c_input[first_row : first_row + CH]
        step_blk = step_size[first_row : first_row + CH]
        cum_block = jnp.cumsum(decay_rate[first_row : first_row + CH], axis=0)
        scores = jnp.einsum("tgn,sgn->gts", c_blk, b_blk, preferred_element_type=jnp.float32)
        cum_gap = cum_block[:, None] - cum_block[None, :]
        weight = (
            jnp.where(causal[:, :, None, None], jnp.exp(jnp.minimum(cum_gap, 0.0)), 0.0)
            * step_blk[None]
        )
        mixing = (weight * jnp.transpose(scores, (1, 2, 0))[:, :, :, None]).astype(jnp.bfloat16)
        intra_parts.append(
            jnp.einsum("tsgr,sgrp->tgrp", mixing, inner_blk, preferred_element_type=jnp.float32)
        )
        cum_parts.append(cum_block)
        local_starts.append(running)
        block_total = cum_block[-1]
        block_totals.append(block_total)
        carry_weight = jnp.exp(block_total[None] - cum_block) * step_blk
        weighted = (inner_blk.astype(jnp.float32) * carry_weight[..., None]).astype(jnp.bfloat16)
        running = jnp.exp(block_total)[..., None, None] * running + jnp.einsum(
            "sgrp,sgn->grpn", weighted, b_blk, preferred_element_type=jnp.float32
        )
    section_decay = block_totals[0]
    block_index = 1
    section_decay = section_decay + block_totals[block_index]

    def combine(earlier, later):
        return (earlier[0] + later[0], jnp.exp(later[0])[..., None, None] * earlier[1] + later[1])

    identity = (jnp.zeros_like(section_decay), jnp.zeros_like(running))
    incoming = entering((section_decay, running), "seq", combine, identity)[1]
    global_starts = []
    ssd_parts = []
    prior_decay = jnp.zeros_like(section_decay)
    for block_index in range(blocks):
        start_state = local_starts[block_index] + jnp.exp(prior_decay)[..., None, None] * incoming
        global_starts.append(start_state)
        prior_decay = prior_decay + block_totals[block_index]
        first_row = block_index * CH
        c_blk = c_input[first_row : first_row + CH]
        outer_part = jnp.exp(cum_parts[block_index])[..., None] * jnp.einsum(
            "tgn,grpn->tgrp", c_blk.astype(jnp.float32), start_state, precision=HIGHEST_PRECISION
        )
        ssd_parts.append(intra_parts[block_index] + outer_part)
    ssd = jnp.concatenate(ssd_parts, axis=0) + skip_gain.reshape(local_groups, group_heads)[
        None, :, :, None
    ] * inner_conv.astype(jnp.float32)
    gated = ssd * jax.nn.silu(gate_raw.astype(jnp.float32))
    local_square = jnp.sum(gated * gated, axis=(2, 3))
    placed = lax.dynamic_update_slice_in_dim(
        jnp.zeros((row_count, G), jnp.float32), local_square, first_group, 1
    )
    square_total = lax.psum(placed, "heads")
    square_mean = lax.dynamic_slice_in_dim(square_total, first_group, local_groups, 1) / (
        per_group * P_SIZE
    )
    normed = (
        gated
        * lax.rsqrt(square_mean + EPSILON)[:, :, None, None]
        * norm_gain.reshape(local_groups, group_heads, P_SIZE)[None]
    )
    mixed = normed.astype(jnp.bfloat16).reshape(row_count, local_heads * P_SIZE)
    cum_all = jnp.concatenate(cum_parts, axis=0)
    starts_all = jnp.stack(global_starts, axis=0)
    positions = lax.broadcasted_iota(jnp.int32, (row_count,), 0)
    bound_local = (
        lax.dynamic_slice_in_dim(step_bounds, section * head_devices, head_devices, 0)
        - section * row_count
    )
    reader_local = lax.dynamic_slice_in_dim(readers, section * head_devices, head_devices, 0)
    block_of = bound_local // CH
    cum_at = cum_all[bound_local]
    inside_mask = (positions[None, :] // CH == block_of[:, None]) & (
        positions[None, :] <= bound_local[:, None]
    )
    cum_gap = cum_at[:, None] - cum_all[None]
    bound_weight = (
        jnp.where(inside_mask[:, :, None, None], jnp.exp(jnp.minimum(cum_gap, 0.0)), 0.0)
        * step_size[None]
    )
    bound_weighted = (inner_conv[None].astype(jnp.float32) * bound_weight[..., None]).astype(
        jnp.bfloat16
    )
    inside = jnp.einsum(
        "bsgrp,sgn->bgrpn", bound_weighted, b_input, preferred_element_type=jnp.float32
    )
    states = jnp.exp(cum_at)[..., None, None] * starts_all[block_of] + inside
    inverse = jnp.argsort(reader_local)
    ordered = states[inverse].reshape(head_devices, local_heads, P_SIZE, N).astype(jnp.bfloat16)
    arrived = lax.all_to_all(
        lax.all_to_all(ordered, "heads", split_axis=0, concat_axis=1, tiled=True),
        "seq",
        split_axis=1,
        concat_axis=0,
        tiled=True,
    )
    return (mixed, arrived[None])


def solution(mesh):
    in_specs = (
        P(("groups", "seq"), "heads"),
        P(None, ("heads", "seq")),
        P(None, "heads"),
        P(None, "heads"),
        P("heads"),
        P("heads"),
        P("heads"),
        P(None, "heads"),
        P("heads"),
        P(),
        P(),
        P("heads"),
        P("groups"),
        P("groups"),
    )
    out_specs = (P(("groups", "seq"), "heads"), P(("groups", "heads"), None, "seq", None, None))
    return jax.shard_map(shards, mesh=mesh, in_specs=in_specs, out_specs=out_specs, check_vma=False)
```

profile of v0, /device:TPU:6, one launch (start us, length us, event | category | flops | bytes accessed | tf_op | source)
XLA Modules:
  0.0 1423.1 jit_solution(13541814008040680989)
XLA Ops:
  8.0 152.5 %all-gather.6.cloned.1.call-done = bf16[512,8192]{1,0:T(8,128)(2,1)} async-done(((bf16[512,2048]{1,0:T(8,128)(2,1)}), bf16[512,8192]{1,0:T(8,128)(2,1)}) %all-gather.6.cloned.1.call-update) | async-done | bytes 8388624 | tf_op jit(solution)/shard_map/all_gather | solution.py:69
  160.4 11.0 convolution_convert_fusion.1
  174.8 6.4 compare_select_fusion
  186.0 29.8 %all-gather.10.cloned.1.call-done = bf16[512,2048]{1,0:T(8,128)(2,1)} async-done(((bf16[512,512]{1,0:T(8,128)(2,1)}), bf16[512,2048]{1,0:T(8,128)(2,1)}) %all-gather.10.cloned.1.call-update) | async-done | bytes 2097168 | tf_op jit(solution)/shard_map/all_gather | solution.py:81
  216.8 773.5 %all-gather.8.cloned.1.call-done = bf16[8192,8192]{1,0:T(8,128)(2,1)} async-done(((bf16[8192,2048]{1,0:T(8,128)(2,1)}), bf16[8192,8192]{1,0:T(8,128)(2,1)}) %all-gather.8.cloned.1.call-update) | async-done | bytes 134217744 | tf_op jit(solution)/shard_map/all_gather | solution.py:73
  990.4 79.7 %convolution_convert_fusion = bf16[512,8192]{1,0:T(8,128)(2,1)} fusion(bf16[512,8192]{1,0:T(8,128)(2,1)} %all-gather.6.cloned.1.call-done, bf16[8192,8192]{1,0:T(8,128)(2,1)} %all-gather.8.cloned.1.call-done), kind=kOutput, calls=%fused_computation.11 | convolution fusion | flops 68723671040 | bytes 150994944 | tf_op jit(solution)/shard_map/dot_general | solution.py:71
  1070.1 12.0 copy.125
  1082.1 7.6 slice_convert_fusion
  1089.7 6.3 copy.101
  1108.6 10.7 multiply_convert_fusion.6
  1127.3 5.1 all_gather.22
  1134.7 48.9 %all-gather.12.cloned.1.call-done = f32[8,32,64,128]{3,2,1,0:T(8,128)} async-done(((f32[2,32,64,128]{3,2,1,0:T(8,128)}), f32[8,32,64,128]{3,2,1,0:T(8,128)}) %all-gather.12.cloned.1.call-update) | async-done | bytes 8388624 | tf_op jit(solution)/shard_map/all_gather | solution.py:25
  1190.1 5.5 fusion.42
  1201.7 6.8 gather_fusion.1
  1208.6 7.2 fusion.31
  1215.9 6.8 fusion.32
  1222.8 14.6 %fusion.15 = (f32[512,2]{0,1:T(2,128)S(1)}, f32[512,4096]{0,1:T(8,128)}) fusion(f32[256,2,32,64]{0,3,2,1:T(8,128)S(1)} %fusion.31, f32[256,2,32,64]{0,3,2,1:T(8,128)} %fusion.32, f32[512,2,32,64]{0,3,2,1:T(8,128)} %bitcast.150, f32[2,32]{1,0:T(2,128)S(1)} %mul.366, f32[515,4096]{0,1:T(8,128)S(1)} %bitcast.147, f32[4096]{0:T(1024)S(1)} %bitcast.176, ...), kind=kLoop, calls=%fused_computation.30 | loop fusion | flops 50330624 | bytes 58806528 | tf_op jit(solution)/shard_map/reduce_sum | solution.py:162
  1237.5 9.6 bitcast_add_fusion.1
  1247.1 5.3 gather_fusion.2
  1252.4 99.6 %all_to_all.24 = bf16[4,64,64,128]{3,2,1,0:T(8,128)(2,1)} all-to-all(bf16[4,64,64,128]{3,2,1,0:T(8,128)(2,1)} %bitcast.155), channel_id=1, replica_groups=mesh['groups'=2,'seq'=4,'heads'=4] {'heads'}, dimensions={0} | all-to-all | bytes 8388608 | tf_op jit(solution)/shard_map/all_to_all | solution.py:204
  1357.1 17.2 %psum.7 = f32[512,8]{0,1:T(8,128)S(1)} all-reduce(f32[512,8]{0,1:T(8,128)S(1)} %dynamic_update_slice.3), channel_id=1, replica_groups=mesh['groups'=2,'seq'=4,'heads'=4] {'heads'}, use_global_device_ids=true, to_apply=%region_7.8 | all-reduce | flops 4096 | bytes 32768 | tf_op jit(solution)/shard_map/psum | solution.py:166
  1374.4 30.4 %fusion.12 = bf16[512,4096]{0,1:T(8,128)(2,1)} fusion(f32[256,4096]{0,1:T(8,128)} %bitcast.156, f32[256,4096]{0,1:T(8,128)} %bitcast.157, f32[512,64,64]{0,2,1:T(8,128)} %get-tuple-element.76, f32[4096]{0:T(1024)S(1)} %copy-done.29, f32[512,2]{0,1:T(2,128)S(1)} %add_rsqrt_fusion, f32[4096]{0:T(1024)S(1)} %mul.368, f32[515,4096]{0,1:T(8,128)} %copy-done.2, ...), kind=kLoop, calls=%fused_computation.26 | loop fusion | flops 52428800 | bytes 54644736 | tf_op jit(solution)/shard_map/convert_element_type | solution.py:175
  1404.8 6.3 copy.119
  1411.1 5.2 copy.181
  (168 shorter events, 54.0 us)
Async XLA Ops:
  7.2 167.6 %copy-start = (bf16[8192,64]{0,1:T(8,128)(2,1)S(1)}, bf16[8192,64]{0,1:T(8,128)(2,1)}, u32[]{:S(2)}) copy-start(bf16[8192,64]{0,1:T(8,128)(2,1)} %param.19) | copy-start | bytes 3145732
  7.2 153.3 %all-gather.6.cloned.1.call-start = ((), (), s32[]{:S(2)}) async-start(), calls=%async_computation.2 | async-start | bytes 10485760 | tf_op jit(solution)/shard_map/all_gather | solution.py:69
  7.9 207.9 %all-gather.10.cloned.1.call-start = ((), (), s32[]{:S(2)}) async-start(), calls=%async_computation.4 | async-start | bytes 2621440 | tf_op jit(solution)/shard_map/all_gather | solution.py:81
  171.6 818.8 %all-gather.8.cloned.1.call-start = ((), (), s32[]{:S(2)}) async-start(), calls=%async_computation.3 | async-start | bytes 167772160 | tf_op jit(solution)/shard_map/all_gather | solution.py:73
  172.3 1011.3 %all-gather.12.cloned.1.call-start = ((), (), s32[]{:S(2)}) async-start(), calls=%async_computation.5 | async-start | bytes 10485760 | tf_op jit(solution)/shard_map/all_gather | solution.py:25
  174.8 933.8 %copy-start.16 = (f32[1,4096]{1,0:T(1,128)}, f32[1,4096]{1,0:T(1,128)S(1)}, u32[]{:S(2)}) copy-start(f32[1,4096]{1,0:T(1,128)S(1)} %get-tuple-element.96) | copy-start | bytes 49156
  174.8 933.8 %copy-start.18 = (f32[1,4096]{1,0:T(1,128)}, f32[1,4096]{1,0:T(1,128)S(1)}, u32[]{:S(2)}) copy-start(f32[1,4096]{1,0:T(1,128)S(1)} %get-tuple-element.97) | copy-start | bytes 49156
  174.8 933.8 %copy-start.20 = (f32[1,4096]{1,0:T(1,128)}, f32[1,4096]{1,0:T(1,128)S(1)}, u32[]{:S(2)}) copy-start(f32[1,4096]{1,0:T(1,128)S(1)} %get-tuple-element.98) | copy-start | bytes 49156
  184.5 885.6 %copy-start.12 = (f32[256,64]{0,1:T(8,128)}, f32[256,64]{0,1:T(8,128)S(1)}, u32[]{:S(2)}) copy-start(f32[256,64]{0,1:T(8,128)S(1)} %get-tuple-element.85) | copy-start | bytes 196612
  184.5 885.6 %copy-start.14 = (f32[256,64]{0,1:T(8,128)}, f32[256,64]{0,1:T(8,128)S(1)}, u32[]{:S(2)}) copy-start(f32[256,64]{0,1:T(8,128)S(1)} %get-tuple-element.84) | copy-start | bytes 196612
  1096.9 5.3 collective-permute-start
  1099.8 22.0 %copy-start.27 = (f32[2,32]{1,0:T(2,128)}, f32[2,32]{1,0:T(2,128)S(1)}, u32[]{:S(2)}) copy-start(f32[2,32]{1,0:T(2,128)S(1)} %get-tuple-element.104) | copy-start | bytes 772
  1103.1 29.5 %copy-start.10 = (bf16[512,2,256]{2,1,0:T(2,128)(2,1)}, bf16[512,2,256]{2,1,0:T(2,128)(2,1)S(1)}, u32[]{:S(2)}) copy-start(bf16[512,2,256]{2,1,0:T(2,128)(2,1)S(1)} %reshape.225) | copy-start | bytes 1572868
  1108.6 10.8 copy-start.2
  1208.6 7.2 copy-start.6
  1208.6 7.2 copy-start.9
  1208.6 7.2 copy-start.11
  1208.6 7.2 copy-start.13
  1208.6 7.2 copy-start.25
  1215.8 7.0 copy-start.4
  1222.8 14.6 %slice-start.3 = ((bf16[512,2,256]{2,1,0:T(2,128)(2,1)}), bf16[512,2,128]{2,1,0:T(2,128)(2,1)S(1)}, s32[]{:S(2)}) async-start(bf16[512,2,256]{2,1,0:T(2,128)(2,1)} %copy-done.10), calls=%async_computation.9 | async-start | bytes 524288 | tf_op jit(solution)/shard_map/slice | solution.py:95
  1252.4 122.0 %copy-start.29 = (f32[4096]{0:T(1024)S(1)}, f32[4096]{0:T(1024)}, u32[]{:S(2)}) copy-start(f32[4096]{0:T(1024)} %param.27) | copy-start | bytes 49156
  1352.0 59.1 %all-to-all-start.1 = ((bf16[1,256,64,128]{3,2,0,1:T(8,128)(2,1)}), bf16[1,256,64,128]{3,2,0,1:T(8,128)(2,1)}, u32[]{:S(2)}, u32[]{:S(2)}) async-start(bf16[1,256,64,128]{3,2,0,1:T(8,128)(2,1)} %bitcast.154), calls=%async_computation.1 | async-start | bytes 8388608 | tf_op jit(solution)/shard_map/all_to_all | solution.py:203
  1374.4 41.9 %copy-start.1 = (bf16[8192,64]{0,1:T(8,128)(2,1)S(1)}, bf16[8192,64]{0,1:T(8,128)(2,1)}, u32[]{:S(2)}) copy-start(bf16[8192,64]{0,1:T(8,128)(2,1)} %param.19) | copy-start | bytes 3145732
  (22 other events, 112.5 us)
Sparse Core Ops, SparseCore 0:
  9.6 150.8 all-gather.5
  171.6 44.0 all-gather.9
  217.3 772.9 all-gather.7
  1125.3 58.2 all-gather.11
where the time goes:
time: 1430 us; the launch traced here: 1420 us
  waiting for transfers between devices  1010 us (71%)
  matrix products  135 us (9%)
  blocking collectives  122 us (9%)
  other arithmetic  83.8 us (6%)
  local copies, waits for them, and re-layouts  50.9 us (4%)
  between operations  14.8 us (1%)
    all_gather x1, waiting for transfers between devices, shards(): lax.all_gather(xz_weight, 'seq', axis=1, tiled=True)  774 us
    all_gather x1, waiting for transfers between devices, shards(): gathered = lax.all_gather(tokens, 'heads', axis=1, tiled=True)  152 us
    all_to_all x1, blocking collectives, shards(): lax.all_to_all(ordered, 'heads', split_axis=0, concat_axis=1, tiled=True)  99.6 us
    dot_general x1, matrix products, shards(): jnp.dot(gathered, lax.all_gather(xz_weight, 'seq', axis=1, tiled=True), p...  79.7 us
    all_gather x1, waiting for transfers between devices, entering(): gathered = jax.tree.map(lambda a: lax.all_gather(a, axis), part)  48.9 us
    convert_element_type x1, other arithmetic, shards(): mixed = normed.astype(jnp.bfloat16).reshape(row_count, local_heads * P_SIZE)  30.4 us
    all_gather x1, waiting for transfers between devices, shards(): bc_every = lax.all_gather(bc_part, 'heads', axis=1, tiled=True)  29.8 us
  transfers between devices with their start and end apart: 6, of which 5 were waited for; matrix products, arithmetic and copies ran while one was open for 4% of the time, Pallas kernels for 0%

commit v1 on v0

v1 whole, which is shorter than its diff:
```python
import jax
import jax.numpy as jnp
from jax import lax
from jax.sharding import PartitionSpec as P

H = 256
P_SIZE = 64
N = 128
G = 8
CH = 256
PER_GROUP = H // G
EPSILON = 1e-05


def conv_rows(raw_rows, kernel, shift_bias):
    row_count = raw_rows.shape[0]
    taps = kernel.shape[0]
    padded = jnp.pad(raw_rows, ((taps - 1, 0), (0, 0))).astype(jnp.float32)
    summed = jnp.broadcast_to(shift_bias[None, :], raw_rows.shape)
    for tap_index in range(taps):
        summed = summed + kernel[tap_index][None, :] * padded[tap_index : tap_index + row_count]
    return jax.nn.silu(summed).astype(jnp.bfloat16)


def project(tokens, xz_weight, bc_weight, step_weight, chunks):
    rows = tokens.shape[0] // chunks
    xz, bc, step = [], [], []
    for c in range(chunks):
        part = lax.all_gather(tokens[c * rows : (c + 1) * rows], "heads", axis=1, tiled=True)
        part = lax.all_gather(part, "seq", axis=0)
        dot = lambda w: lax.dot_general(
            part, w, (((2,), (0,)), ((), ())), preferred_element_type=jnp.float32
        )
        xz.append(dot(xz_weight).astype(jnp.bfloat16))
        bc.append(dot(bc_weight).astype(jnp.bfloat16))
        step.append(dot(step_weight))
    whole = lambda parts: jnp.stack(parts, axis=1).reshape(-1, parts[0].shape[-1])
    return whole(xz), whole(bc), whole(step)


def shards(
    tokens,
    xz_weight,
    bc_weight,
    step_weight,
    step_bias,
    decay_log,
    skip_gain,
    conv_weight,
    conv_bias,
    bc_conv_weight,
    bc_conv_bias,
    norm_gain,
    step_bounds,
    readers,
):
    head_devices = lax.axis_size("heads")
    sections = lax.axis_size("seq")
    section = lax.axis_index("seq")
    head_block = lax.axis_index("heads")
    block_heads = H // head_devices
    mine = block_heads // sections
    first_mine = section * mine
    group = (head_block * block_heads + first_mine) // PER_GROUP
    own = lambda a, width, axis: lax.dynamic_slice_in_dim(a, first_mine * width, mine * width, axis)
    width_bc = bc_weight.shape[1]
    whole_group = width_bc >= 2 * N
    if whole_group:
        first_col = group * 2 * N - head_block * width_bc
        bc_weight = lax.dynamic_slice_in_dim(bc_weight, first_col, 2 * N, 1)
    xz, bc_raw, step_raw = project(
        tokens, xz_weight, bc_weight, own(step_weight, 1, 1), 4
    )
    if not whole_group:
        bc_raw = lax.all_gather(bc_raw, "heads", axis=1, tiled=True)
        bc_raw = lax.dynamic_slice_in_dim(bc_raw, group * 2 * N, 2 * N, 1)
    length = xz.shape[0]
    blocks = length // CH
    xz = xz.reshape(length, mine, 2, P_SIZE)
    inner_raw = xz[:, :, 0].reshape(length, mine * P_SIZE)
    gate_raw = xz[:, :, 1]
    inner = conv_rows(inner_raw, own(conv_weight, P_SIZE, 1), own(conv_bias, P_SIZE, 0)).reshape(
        blocks, CH, mine, P_SIZE
    )
    bc = conv_rows(
        bc_raw,
        lax.dynamic_slice_in_dim(bc_conv_weight, group * 2 * N, 2 * N, 1),
        lax.dynamic_slice_in_dim(bc_conv_bias, group * 2 * N, 2 * N, 0),
    ).reshape(blocks, CH, 2 * N)
    b_input, c_input = bc[:, :, :N], bc[:, :, N:]
    step_size = jax.nn.softplus(step_raw + own(step_bias, 1, 0)[None]).reshape(blocks, CH, mine)
    decay = -jnp.exp(own(decay_log, 1, 0))[None, None] * step_size
    cum = jnp.cumsum(decay, axis=1)
    total = cum[:, -1]
    causal = lax.broadcasted_iota(jnp.int32, (CH, CH), 0) >= lax.broadcasted_iota(
        jnp.int32, (CH, CH), 1
    )
    carry_weight = jnp.exp(total[:, None] - cum) * step_size
    inner_f = inner.astype(jnp.float32)
    weighted = (inner_f * carry_weight[..., None]).astype(jnp.bfloat16)
    added = jnp.einsum("cshp,csn->chpn", weighted, b_input, preferred_element_type=jnp.float32)
    starts = [jnp.zeros_like(added[0])]
    for c in range(blocks - 1):
        starts.append(jnp.exp(total[c])[:, None, None] * starts[-1] + added[c])
    starts = jnp.stack(starts)
    scores = jnp.einsum("ctn,csn->cts", c_input, b_input, preferred_element_type=jnp.float32)
    cum_h = jnp.transpose(cum, (0, 2, 1))
    step_h = jnp.transpose(step_size, (0, 2, 1))
    gap = cum_h[:, :, :, None] - cum_h[:, :, None, :]
    mixing = (
        jnp.where(causal, jnp.exp(jnp.minimum(gap, 0.0)), 0.0)
        * step_h[:, :, None, :]
        * scores[:, None]
    ).astype(jnp.bfloat16)
    intra = jnp.einsum("chts,cshp->cthp", mixing, inner, preferred_element_type=jnp.float32)
    outer = jnp.exp(cum)[..., None] * jnp.einsum(
        "ctn,chpn->cthp", c_input, starts.astype(jnp.bfloat16), preferred_element_type=jnp.float32
    )
    ssd = intra + outer + own(skip_gain, 1, 0)[:, None] * inner_f
    gated = ssd.reshape(length, mine, P_SIZE) * jax.nn.silu(gate_raw.astype(jnp.float32))

    bounds_per = step_bounds.shape[0] // sections
    order = jnp.argsort(readers.reshape(sections, bounds_per), axis=1)
    ordered = jnp.take_along_axis(step_bounds.reshape(sections, bounds_per), order, axis=1)
    positions = jnp.transpose(ordered).reshape(-1)
    block_of = positions // CH
    offset = positions % CH
    cum_b = cum[block_of]
    cum_at = jnp.take_along_axis(cum_b, offset[:, None, None], axis=1)
    inside_mask = lax.broadcasted_iota(jnp.int32, (1, CH), 1) <= offset[:, None]
    bound_weight = (
        jnp.where(inside_mask[:, :, None], jnp.exp(jnp.minimum(cum_at - cum_b, 0.0)), 0.0)
        * step_size[block_of]
    )
    bound_weighted = (inner_f[block_of] * bound_weight[..., None]).astype(jnp.bfloat16)
    inside = jnp.einsum(
        "bshp,bsn->bhpn", bound_weighted, b_input[block_of], preferred_element_type=jnp.float32
    )
    states = jnp.exp(cum_at[:, 0])[..., None, None] * starts[block_of] + inside
    states = states.astype(jnp.bfloat16).reshape(bounds_per, sections, mine, P_SIZE, N)

    sub = head_devices // sections
    rank = section * sub + head_block % sub
    pieces = []
    for d in range(head_devices):
        pairs = [
            (s * head_devices + k, (k // sub) * head_devices + (s * sub + k % sub + d) % head_devices)
            for s in range(sections)
            for k in range(head_devices)
        ]
        piece = lax.dynamic_index_in_dim(states, (rank + d) % head_devices, 0, False)
        pieces.append(lax.ppermute(piece, ("seq", "heads"), pairs))
    stacked = jnp.stack(pieces)
    source = jnp.arange(head_devices)
    by_rank = jnp.take(stacked, (head_block - source) % head_devices, axis=0)
    by_rank = by_rank.reshape(sections, sub, sections, mine, P_SIZE, N)
    handoff = jnp.transpose(by_rank, (2, 1, 0, 3, 4, 5)).reshape(
        1, sections, sub * sections * mine, P_SIZE, N
    )

    gated = gated.astype(jnp.bfloat16).reshape(length, mine * P_SIZE)
    gated = lax.all_to_all(gated, "seq", split_axis=0, concat_axis=1, tiled=True)
    gated = gated.astype(jnp.float32)
    row_count = gated.shape[0]
    local_groups = max(1, block_heads // PER_GROUP)
    square = jnp.sum(jnp.square(gated.reshape(row_count, local_groups, -1)), axis=2)
    if block_heads < PER_GROUP:
        first_group = head_block * block_heads // PER_GROUP
        placed = lax.dynamic_update_slice_in_dim(
            jnp.zeros((row_count, G), jnp.float32), square, first_group, 1
        )
        square = lax.dynamic_slice_in_dim(lax.psum(placed, "heads"), first_group, 1, 1)
    scale = lax.rsqrt(square / (PER_GROUP * P_SIZE) + EPSILON)
    normed = gated.reshape(row_count, local_groups, -1) * scale[:, :, None]
    mixed = normed.reshape(row_count, -1) * norm_gain[None]
    return (mixed.astype(jnp.bfloat16), handoff)


def solution(mesh):
    in_specs = (
        P(("groups", "seq"), "heads"),
        P(None, ("heads", "seq")),
        P(None, "heads"),
        P(None, "heads"),
        P("heads"),
        P("heads"),
        P("heads"),
        P(None, "heads"),
        P("heads"),
        P(),
        P(),
        P("heads"),
        P("groups"),
        P("groups"),
    )
    out_specs = (P(("groups", "seq"), "heads"), P(("groups", "heads"), None, "seq", None, None))
    return jax.shard_map(shards, mesh=mesh, in_specs=in_specs, out_specs=out_specs, check_vma=False)
```

time: 1430 us -> 812 us (0.57)
  waiting for transfers between devices: 1010 us -> 415 us
  blocking collectives: 122 us -> 0 us
  local copies, waits for them, and re-layouts: 50.9 us -> 119 us
  matrix products: 135 us -> 177 us
  other arithmetic: 83.8 us -> 61.2 us
    all_gather x4 -> x8, waiting for transfers between devices: 1000 us -> 324 us  [the longest x4 172 us: project(): lax.all_gather(tokens[c * rows:(c + 1) * rows], 'heads', axis=1, tiled=True)]
    all_to_all x1 -> x0, blocking collectives: 99.6 us -> none  [shards(): lax.all_to_all(ordered, 'heads', split_axis=0, concat_axis=1, tiled=True)]
    ppermute x1 -> x4, waiting for transfers between devices: 2.35 us -> 88.8 us  [shards(): pieces.append(lax.ppermute(piece, ('seq', 'heads'), pairs))]
    dot_general x12 -> x17, matrix products: 135 us -> 177 us  [the longest x12 141 us: project(): lax.dot_general(part, w, (((2,), (0,)), ((), ())), preferred_element_type...]
    another operation x8 -> x7, local copies, waits for them, and re-layouts: 0.46 us -> 29.2 us  [the longest x3 14.7 us: project(): jnp.stack(parts, axis=1).reshape(-1, parts[0].shape[-1])]
    convert_element_type x4 -> x6, other arithmetic: 42.6 us -> 25.3 us  [the longest x1 8.11 us: shards(): gated = gated.astype(jnp.bfloat16).reshape(length, mine * P_SIZE)]
    psum x1 -> x0, blocking collectives: 17.2 us -> none  [shards(): square_total = lax.psum(placed, 'heads')]
    gather x3 -> x13, local copies, waits for them, and re-layouts: 12.7 us -> 29.3 us  [the longest x1 11.2 us: shards(): inner_f[block_of] * bound_weight[..., None]]
  transfers between devices with their start and end apart: 6 -> 13, of which waited for: 5 -> 10; matrix products, arithmetic and copies ran while one was open for 4% -> 20% of each run, Pallas kernels for 0% -> 0%
where the time goes in v1:
time: 812 us; the launch traced here: 801 us
  waiting for transfers between devices  415 us (51%)
  matrix products  177 us (22%)
  local copies, waits for them, and re-layouts  119 us (15%)
  other arithmetic  61.2 us (8%)
  between operations  15.2 us (2%)
  starting transfers between devices  14.4 us (2%)
    all_gather x4, waiting for transfers between devices, project(): lax.all_gather(tokens[c * rows:(c + 1) * rows], 'heads', axis=1, tiled=True)  172 us
    all_gather x4, waiting for transfers between devices, project(): part = lax.all_gather(part, 'seq', axis=0)  152 us
    dot_general x12, matrix products, project(): lax.dot_general(part, w, (((2,), (0,)), ((), ())), preferred_element_type...  141 us
    ppermute x4, waiting for transfers between devices, shards(): pieces.append(lax.ppermute(piece, ('seq', 'heads'), pairs))  88.8 us
    dot_general x1, matrix products, shards(): jnp.einsum('chts,cshp->cthp', mixing, inner, preferred_element_type=jnp.f...  18.5 us
  transfers between devices with their start and end apart: 13, of which 10 were waited for; matrix products, arithmetic and copies ran while one was open for 20% of the time, Pallas kernels for 0%

profile of v1, /device:TPU:6, one launch (start us, length us, event | category | flops | bytes accessed | tf_op | source)
XLA Modules:
  0.0 801.0 jit_solution(14985137728588360591)
XLA Ops:
  12.4 45.1 %all-gather.17.cloned.1.call-done = bf16[128,8192]{1,0:T(8,128)(2,1)} async-done(((bf16[128,2048]{1,0:T(8,128)(2,1)}), bf16[128,8192]{1,0:T(8,128)(2,1)}) %all-gather.17.cloned.1.call-update) | async-done | bytes 2097168 | tf_op jit(solution)/shard_map/all_gather | solution.py:29
  57.6 46.2 %all-gather.19.cloned.1.call-done = bf16[128,8192]{1,0:T(8,128)(2,1)} async-done(((bf16[128,2048]{1,0:T(8,128)(2,1)}), bf16[128,8192]{1,0:T(8,128)(2,1)}) %all-gather.19.cloned.1.call-update) | async-done | bytes 2097168 | tf_op jit(solution)/shard_map/all_gather | solution.py:29
  103.8 46.8 %all-gather.15.cloned.1.call-done = bf16[128,8192]{1,0:T(8,128)(2,1)} async-done(((bf16[128,2048]{1,0:T(8,128)(2,1)}), bf16[128,8192]{1,0:T(8,128)(2,1)}) %all-gather.15.cloned.1.call-update) | async-done | bytes 2097168 | tf_op jit(solution)/shard_map/all_gather | solution.py:29
  163.1 34.2 %all-gather.13.cloned.1.call-done = bf16[128,8192]{1,0:T(8,128)(2,1)} async-done(((bf16[128,2048]{1,0:T(8,128)(2,1)}), bf16[128,8192]{1,0:T(8,128)(2,1)}) %all-gather.13.cloned.1.call-update) | async-done | bytes 2097168 | tf_op jit(solution)/shard_map/all_gather | solution.py:29
  197.3 57.5 %all-gather.25.cloned.1.call-done = bf16[512,8192]{1,0:T(8,128)(2,1)} async-done(((bf16[128,8192]{1,0:T(8,128)(2,1)}), bf16[512,8192]{1,0:T(8,128)(2,1)}) %all-gather.25.cloned.1.call-update) | async-done | bytes 8388624 | tf_op jit(solution)/shard_map/all_gather | solution.py:30
  261.1 53.5 %all-gather.27.cloned.1.call-done = bf16[512,8192]{1,0:T(8,128)(2,1)} async-done(((bf16[128,8192]{1,0:T(8,128)(2,1)}), bf16[512,8192]{1,0:T(8,128)(2,1)}) %all-gather.27.cloned.1.call-update) | async-done | bytes 8388624 | tf_op jit(solution)/shard_map/all_gather | solution.py:30
  321.0 9.0 %fusion.89 = bf16[4,1,128,256]{3,2,0,1:T(8,128)(2,1)} fusion(bf16[4,128,8192]{2,1,0:T(8,128)(2,1)} %bitcast.247, bf16[8192,512]{1,0:T(8,128)(2,1)} %param.16, s32[]{:T(128)S(6)} %select_n.209), kind=kOutput, calls=%fused_computation.95 | convolution fusion | flops 2147614720 | bytes 12845060 | tf_op jit(solution)/shard_map/dot_general | solution.py:31
  334.0 40.5 %all-gather.23.cloned.1.call-done = bf16[512,8192]{1,0:T(8,128)(2,1)} async-done(((bf16[128,8192]{1,0:T(8,128)(2,1)}), bf16[512,8192]{1,0:T(8,128)(2,1)}) %all-gather.23.cloned.1.call-update) | async-done | bytes 8388624 | tf_op jit(solution)/shard_map/all_gather | solution.py:30
  386.8 23.9 %fusion.55 = bf16[4,1,128,2048]{3,2,0,1:T(8,128)(2,1)} fusion(bf16[4,128,8192]{2,1,0:T(8,128)(2,1)S(1)} %bitcast.250, bf16[8192,2048]{1,0:T(8,128)(2,1)} %param.15), kind=kOutput, calls=%fused_computation.72 | convolution fusion | flops 17180917760 | bytes 44040192 | tf_op jit(solution)/shard_map/dot_general | solution.py:31
  410.8 22.5 %fusion.52 = bf16[4,1,128,2048]{3,2,0,1:T(8,128)(2,1)} fusion(bf16[4,128,8192]{2,1,0:T(8,128)(2,1)S(1)} %bitcast.257, bf16[8192,2048]{1,0:T(8,128)(2,1)} %param.15), kind=kOutput, calls=%fused_computation.71 | convolution fusion | flops 17180917760 | bytes 44040192 | tf_op jit(solution)/shard_map/dot_general | solution.py:31
  433.3 24.6 %fusion.58 = bf16[4,1,128,2048]{3,2,0,1:T(8,128)(2,1)} fusion(bf16[4,128,8192]{2,1,0:T(8,128)(2,1)} %bitcast.259, bf16[8192,2048]{1,0:T(8,128)(2,1)} %param.15), kind=kOutput, calls=%fused_computation.73 | convolution fusion | flops 17180917760 | bytes 44040192 | tf_op jit(solution)/shard_map/dot_general | solution.py:31
  468.3 22.7 %fusion.61 = bf16[4,1,128,2048]{3,2,0,1:T(8,128)(2,1)} fusion(bf16[4,128,8192]{2,1,0:T(8,128)(2,1)S(1)} %bitcast.263, bf16[8192,2048]{1,0:T(8,128)(2,1)} %param.15), kind=kOutput, calls=%fused_computation.74 | convolution fusion | flops 17180917760 | bytes 44040192 | tf_op jit(solution)/shard_map/dot_general | solution.py:31
  509.1 14.5 %copy.77 = bf16[4,4,128,2048]{2,1,0,3:T(4,128)(2,1)} copy(bf16[4,4,128,2048]{3,2,0,1:T(8,128)(2,1)} %pad_maximum_fusion) | data formatting | bytes 16777216 | tf_op jit(solution)/shard_map/stack | solution.py:37
  523.6 14.5 %reshape_reshape.3 = bf16[2048,16,2,64]{0,3,2,1:T(8,128)(2,1)} reshape(bf16[4,4,128,2048]{2,1,0,3:T(4,128)(2,1)} %copy.77) | data formatting | bytes 16777216 | tf_op jit(solution)/shard_map/reshape;reshape | solution.py:79
  546.5 8.4 %multiply_convert_fusion.5 = bf16[2048,1024]{0,1:T(8,128)(2,1)S(1)} fusion(f32[2051,1024]{0,1:T(8,128)S(1)} %pad_convert_fusion, f32[1024]{0:T(1024)S(1)} %bitcast.275, f32[1024]{0:T(1024)S(1)} %bitcast.273, f32[1024]{0:T(1024)S(1)} %bitcast.274, f32[1024]{0:T(1024)S(1)} %bitcast.272, f32[1024]{0:T(1024)S(1)} %dynamic-slice-done), kind=kLoop, calls=%fused_computation.46 | loop fusion | flops 27262976 | bytes 37769216 | tf_op jit(solution)/shard_map/convert_element_type | solution.py:22
  580.1 10.8 %reshape.489 = f32[4,512,1024]{1,0,2:T(4,128)} reshape(f32[2048,16,1,64]{0,3,2,1:T(8,128)} %get-tuple-element.29) | data formatting | bytes 16777216 | tf_op jit(solution)/shard_map/convert_element_type | solution.py:120
  591.0 18.5 %fusion.23 = f32[8,256,16,64]{1,3,2,0:T(8,128)S(1)} fusion(f32[8,256,16,64]{1,3,2,0:T(8,128)} %fusion.72, f32[16]{0:T(128)S(1)} %copy-done.35, f32[8,256,16]{1,2,0:T(8,128)S(1)} %get-tuple-element.41, f32[8,256,256]{2,1,0:T(8,128)} %fusion.104, f32[8,16,256]{2,1,0:T(8,128)S(1)} %bitcast.235, f32[8,16,256]{2,1,0:T(8,128)S(1)} %get-tuple-element.39, ...), kind=kOutput, calls=%fused_computation.41 | convolution fusion | flops 1134559232 | bytes 23527488 | tf_op jit(solution)/shard_map/chts,cshp->cthp/dot_general | solution.py:115
  609.5 9.7 %copy.87 = f32[8,256,16,64]{1,0,3,2:T(8,128)} copy(f32[8,256,16,64]{1,3,2,0:T(8,128)S(1)} %fusion.23) | data formatting | bytes 16777216 | tf_op jit(solution)/shard_map/add | solution.py:119
  619.3 10.6 %reshape.480 = f32[4,512,1024]{1,0,2:T(4,128)} reshape(f32[8,256,16,64]{1,0,3,2:T(8,128)} %copy.87) | data formatting | bytes 16777216 | tf_op jit(solution)/shard_map/reshape | solution.py:120
  629.9 8.1 %fusion.25 = bf16[4,512,1024]{1,0,2:T(4,128)(2,1)S(1)} fusion(f32[4,512,1024]{1,0,2:T(4,128)} %reshape.480, f32[4,512,1024]{1,0,2:T(4,128)} %reshape.489), kind=kLoop, calls=%fused_computation.47 | loop fusion | flops 12582912 | bytes 20971520 | tf_op jit(solution)/shard_map/convert_element_type | solution.py:161
  647.0 11.2 %gather_fusion.2 = f32[16,256,16,64]{1,3,2,0:T(8,128)} fusion(f32[8,256,16,64]{1,3,2,0:T(8,128)} %copy_convert_fusion, s32[1024]{0:T(1024)S(1)} %copy-done.21), kind=kCustom, calls=%fused_computation.2 | custom fusion | bytes 33554496 | tf_op jit(solution)/shard_map/gather | solution.py:135
  659.8 9.5 %add_convert_fusion = bf16[16,16,64,128]{3,2,1,0:T(8,128)(2,1)S(1)} fusion(f32[16,16,64,128]{3,2,1,0:T(8,128)} %gather_fusion.1, f32[16,16]{1,0:T(8,128)S(1)} %get-tuple-element.17, f32[16,256,16,64]{1,3,2,0:T(8,128)} %gather_fusion.2, f32[16,256,16]{1,2,0:T(8,128)S(1)} %select_multiply_fusion, bf16[16,256,128]{2,1,0:T(8,128)(2,1)S(1)} %gather_fusion.4), kind=kOutput, calls=%fused_computation.42 | convolution fusion | flops 1088421888 | bytes 30671872 | tf_op jit(solution)/shard_map/bshp,bsn->bhpn/dot_general | solution.py:136
  678.3 65.8 %collective-permute-done = bf16[4,16,64,128]{3,2,1,0:T(8,128)(2,1)S(1)} collective-permute-done((bf16[4,16,64,128]{3,2,1,0:T(8,128)(2,1)S(1)}, bf16[4,16,64,128]{3,2,1,0:T(8,128)(2,1)S(1)}, u32[]{:S(2)}, u32[]{:S(2)}) %collective-permute-start) | collective-permute-done | bytes 1048608 | tf_op jit(solution)/shard_map/ppermute | solution.py:152
  744.1 22.2 %collective-permute-done.3 = bf16[4,16,64,128]{3,2,1,0:T(8,128)(2,1)S(1)} collective-permute-done((bf16[4,16,64,128]{3,2,1,0:T(8,128)(2,1)S(1)}, bf16[4,16,64,128]{3,2,1,0:T(8,128)(2,1)S(1)}, u32[]{:S(2)}, u32[]{:S(2)}) %collective-permute-start.3) | collective-permute-done | bytes 1048608 | tf_op jit(solution)/shard_map/ppermute | solution.py:152
  (216 shorter events, 155.3 us)
Async XLA Ops:
  7.2 247.7 %copy-start = (bf16[8192,64]{0,1:T(8,128)(2,1)S(1)}, bf16[8192,64]{0,1:T(8,128)(2,1)}, u32[]{:S(2)}) copy-start(bf16[8192,64]{0,1:T(8,128)(2,1)} %param.17) | copy-start | bytes 3145732
  7.2 143.6 %copy-start.29 = (s32[16]{0:T(128)S(1)}, s32[16]{0:T(128)}, u32[]{:S(2)}) copy-start(s32[16]{0:T(128)} %param.26) | copy-start | bytes 196
  7.2 143.7 %copy-start.30 = (s32[16]{0:T(128)S(1)}, s32[16]{0:T(128)}, u32[]{:S(2)}) copy-start(s32[16]{0:T(128)} %param.27) | copy-start | bytes 196
  7.2 145.8 %copy-start.32 = (f32[64]{0:T(128)S(1)}, f32[64]{0:T(128)}, u32[]{:S(2)}) copy-start(f32[64]{0:T(128)} %param.18) | copy-start | bytes 772
  7.2 146.4 %copy-start.33 = (f32[64]{0:T(128)S(1)}, f32[64]{0:T(128)}, u32[]{:S(2)}) copy-start(f32[64]{0:T(128)} %param.20) | copy-start | bytes 772
  7.2 148.4 %copy-start.34 = (f32[64]{0:T(128)S(1)}, f32[64]{0:T(128)}, u32[]{:S(2)}) copy-start(f32[64]{0:T(128)} %param.19) | copy-start | bytes 772
  7.2 50.3 %all-gather.17.cloned.1.call-start = ((), (), s32[]{:S(2)}) async-start(), calls=%async_computation.3 | async-start | bytes 2621440 | tf_op jit(solution)/shard_map/all_gather | solution.py:29
  10.3 93.5 %all-gather.19.cloned.1.call-start = ((), (), s32[]{:S(2)}) async-start(), calls=%async_computation.4 | async-start | bytes 2621440 | tf_op jit(solution)/shard_map/all_gather | solution.py:29
  11.0 139.6 %all-gather.15.cloned.1.call-start = ((), (), s32[]{:S(2)}) async-start(), calls=%async_computation.2 | async-start | bytes 2621440 | tf_op jit(solution)/shard_map/all_gather | solution.py:29
  11.7 185.5 %all-gather.13.cloned.1.call-start = ((), (), s32[]{:S(2)}) async-start(), calls=%async_computation.1 | async-start | bytes 2621440 | tf_op jit(solution)/shard_map/all_gather | solution.py:29
  12.3 242.5 %all-gather.25.cloned.1.call-start = ((), (), s32[]{:S(2)}) async-start(), calls=%async_computation.7 | async-start | bytes 10485760 | tf_op jit(solution)/shard_map/all_gather | solution.py:30
  57.5 257.0 %all-gather.27.cloned.1.call-start = ((), (), s32[]{:S(2)}) async-start(), calls=%async_computation.8 | async-start | bytes 10485760 | tf_op jit(solution)/shard_map/all_gather | solution.py:30
  103.8 270.7 %all-gather.23.cloned.1.call-start = ((), (), s32[]{:S(2)}) async-start(), calls=%async_computation.6 | async-start | bytes 10485760 | tf_op jit(solution)/shard_map/all_gather | solution.py:30
  150.6 307.3 %all-gather.21.cloned.1.call-start = ((), (), s32[]{:S(2)}) async-start(), calls=%async_computation.5 | async-start | bytes 10485760 | tf_op jit(solution)/shard_map/all_gather | solution.py:30
  380.9 29.9 %slice-start.4 = ((s8[8388608]{0:T(1024)(128)(4,1)}), s8[4194304]{0:T(1024)(128)(4,1)S(1)}, s32[]{:S(2)}) async-start(s8[8388608]{0:T(1024)(128)(4,1)} %bitcast.255), calls=%async_computation.13 | async-start | bytes 8388608
  386.8 23.9 %slice-start.5 = ((s8[8388608]{0:T(1024)(128)(4,1)}), s8[4194304]{0:T(1024)(128)(4,1)S(1)}, s32[]{:S(2)}) async-start(s8[8388608]{0:T(1024)(128)(4,1)} %bitcast.255), calls=%async_computation.14 | async-start | bytes 8388608
  468.3 28.7 %copy-start.7 = (bf16[4,1,128,256]{3,2,0,1:T(8,128)(2,1)S(1)}, bf16[4,1,128,256]{3,2,0,1:T(8,128)(2,1)}, u32[]{:S(2)}) copy-start(bf16[4,1,128,256]{3,2,0,1:T(8,128)(2,1)} %fusion.89) | copy-start | bytes 786436
  468.3 28.7 %copy-start.8 = (bf16[4,1,128,256]{3,2,0,1:T(8,128)(2,1)S(1)}, bf16[4,1,128,256]{3,2,0,1:T(8,128)(2,1)}, u32[]{:S(2)}) copy-start(bf16[4,1,128,256]{3,2,0,1:T(8,128)(2,1)} %fusion.86) | copy-start | bytes 786436
  468.3 28.7 %copy-start.9 = (bf16[4,1,128,256]{3,2,0,1:T(8,128)(2,1)S(1)}, bf16[4,1,128,256]{3,2,0,1:T(8,128)(2,1)}, u32[]{:S(2)}) copy-start(bf16[4,1,128,256]{3,2,0,1:T(8,128)(2,1)} %fusion.92) | copy-start | bytes 786436
  640.8 139.5 %all-to-all-start = ((bf16[4,512,1024]{1,2,0:T(8,128)(2,1)}), bf16[4,512,1024]{1,2,0:T(8,128)(2,1)}, u32[]{:S(2)}, u32[]{:S(2)}) async-start(bf16[4,512,1024]{1,2,0:T(8,128)(2,1)} %copy.88), calls=%async_computation | async-start | bytes 8388608 | tf_op jit(solution)/shard_map/all_to_all | solution.py:162
  670.2 73.8 %collective-permute-start = (bf16[4,16,64,128]{3,2,1,0:T(8,128)(2,1)S(1)}, bf16[4,16,64,128]{3,2,1,0:T(8,128)(2,1)S(1)}, u32[]{:S(2)}, u32[]{:S(2)}) collective-permute-start(bf16[4,16,64,128]{3,2,1,0:T(8,128)(2,1)S(1)} %get-tuple-element.31), channel_id=1, source_target_pairs={{0,0},{1,4},{2,8},{3,12},{4,1},{5,5},{6,9},{7,13},{8,2},{9,6},{10,... | collective-permute-start | bytes 3145736 | tf_op jit(solution)/shard_map/ppermute | solution.py:152
  674.0 92.3 %collective-permute-start.3 = (bf16[4,16,64,128]{3,2,1,0:T(8,128)(2,1)S(1)}, bf16[4,16,64,128]{3,2,1,0:T(8,128)(2,1)S(1)}, u32[]{:S(2)}, u32[]{:S(2)}) collective-permute-start(bf16[4,16,64,128]{3,2,1,0:T(8,128)(2,1)S(1)} %get-tuple-element.32), channel_id=1, source_target_pairs={{0,3},{1,7},{2,11},{3,15},{4,0},{5,4},{6,8},{7,12},{8,1},{9,5},{10... | collective-permute-start | bytes 3145736 | tf_op jit(solution)/shard_map/ppermute | solution.py:152
  674.1 93.0 %collective-permute-start.2 = (bf16[4,16,64,128]{3,2,1,0:T(8,128)(2,1)S(1)}, bf16[4,16,64,128]{3,2,1,0:T(8,128)(2,1)S(1)}, u32[]{:S(2)}, u32[]{:S(2)}) collective-permute-start(bf16[4,16,64,128]{3,2,1,0:T(8,128)(2,1)S(1)} %get-tuple-element.33), channel_id=1, source_target_pairs={{0,2},{1,6},{2,10},{3,14},{4,3},{5,7},{6,11},{7,15},{8,0},{9,4},{1... | collective-permute-start | bytes 3145736 | tf_op jit(solution)/shard_map/ppermute | solution.py:152
  677.3 89.9 %collective-permute-start.1 = (bf16[4,16,64,128]{3,2,1,0:T(8,128)(2,1)S(1)}, bf16[4,16,64,128]{3,2,1,0:T(8,128)(2,1)S(1)}, u32[]{:S(2)}, u32[]{:S(2)}) collective-permute-start(bf16[4,16,64,128]{3,2,1,0:T(8,128)(2,1)S(1)} %get-tuple-element.34), channel_id=1, source_target_pairs={{0,1},{1,5},{2,9},{3,13},{4,2},{5,6},{6,10},{7,14},{8,3},{9,7},{10... | collective-permute-start | bytes 3145736 | tf_op jit(solution)/shard_map/ppermute | solution.py:152
  (34 other events, 325.5 us)
Sparse Core Ops, SparseCore 0:
  10.4 47.0 all-gather.16
  59.1 44.6 all-gather.18
  105.9 44.6 all-gather.14
  152.6 44.6 all-gather.12
  198.7 56.0 all-gather.24
  256.3 58.2 all-gather.26
  316.1 58.2 all-gather.22
  376.0 58.2 all-gather.20

commit v2 on v1

--- a/solution.py
+++ b/solution.py
@@ -23,13 +23,18 @@
 
 
 def project(tokens, xz_weight, bc_weight, step_weight, chunks):
+    sections, head_devices = lax.axis_size("seq"), lax.axis_size("heads")
     rows = tokens.shape[0] // chunks
+    width = tokens.shape[1]
     xz, bc, step = [], [], []
     for c in range(chunks):
-        part = lax.all_gather(tokens[c * rows : (c + 1) * rows], "heads", axis=1, tiled=True)
-        part = lax.all_gather(part, "seq", axis=0)
+        part = lax.all_gather(tokens[c * rows : (c + 1) * rows], ("seq", "heads"), axis=0)
+        part = part.reshape(sections, head_devices, rows, width)
         dot = lambda w: lax.dot_general(
-            part, w, (((2,), (0,)), ((), ())), preferred_element_type=jnp.float32
+            part,
+            w.reshape(head_devices, width, w.shape[1]),
+            (((1, 3), (0, 1)), ((), ())),
+            preferred_element_type=jnp.float32,
         )
         xz.append(dot(xz_weight).astype(jnp.bfloat16))
         bc.append(dot(bc_weight).astype(jnp.bfloat16))
@@ -69,7 +74,7 @@
         first_col = group * 2 * N - head_block * width_bc
         bc_weight = lax.dynamic_slice_in_dim(bc_weight, first_col, 2 * N, 1)
     xz, bc_raw, step_raw = project(
-        tokens, xz_weight, bc_weight, own(step_weight, 1, 1), 4
+        tokens, xz_weight, bc_weight, own(step_weight, 1, 1), 2
     )
     if not whole_group:
         bc_raw = lax.all_gather(bc_raw, "heads", axis=1, tiled=True)
@@ -103,6 +108,27 @@
     for c in range(blocks - 1):
         starts.append(jnp.exp(total[c])[:, None, None] * starts[-1] + added[c])
     starts = jnp.stack(starts)
+    bounds_per = step_bounds.shape[0] // sections
+    order = jnp.argsort(readers.reshape(sections, bounds_per), axis=1)
+    ordered = jnp.take_along_axis(step_bounds.reshape(sections, bounds_per), order, axis=1)
+    positions = jnp.transpose(ordered).reshape(-1)
+    block_of = positions // CH
+    offset = positions % CH
+    cum_b = cum[block_of]
+    cum_at = jnp.take_along_axis(cum_b, offset[:, None, None], axis=1)
+    inside_mask = lax.broadcasted_iota(jnp.int32, (1, CH), 1) <= offset[:, None]
+    bound_weight = (
+        jnp.where(inside_mask[:, :, None], jnp.exp(jnp.minimum(cum_at - cum_b, 0.0)), 0.0)
+        * step_size[block_of]
+    )
+    bound_weighted = (inner_f[block_of] * bound_weight[..., None]).astype(jnp.bfloat16)
+    inside = jnp.einsum(
+        "bshp,bsn->bhpn", bound_weighted, b_input[block_of], preferred_element_type=jnp.float32
+    )
+    states = jnp.exp(cum_at[:, 0])[..., None, None] * starts[block_of] + inside
+    states = states.astype(jnp.bfloat16).reshape(bounds_per, sections, mine, P_SIZE, N)
+    states, c_input = lax.optimization_barrier((states, c_input))
+
     scores = jnp.einsum("ctn,csn->cts", c_input, b_input, preferred_element_type=jnp.float32)
     cum_h = jnp.transpose(cum, (0, 2, 1))
     step_h = jnp.transpose(step_size, (0, 2, 1))
@@ -118,26 +144,6 @@
     )
     ssd = intra + outer + own(skip_gain, 1, 0)[:, None] * inner_f
     gated = ssd.reshape(length, mine, P_SIZE) * jax.nn.silu(gate_raw.astype(jnp.float32))
-
-    bounds_per = step_bounds.shape[0] // sections
-    order = jnp.argsort(readers.reshape(sections, bounds_per), axis=1)
-    ordered = jnp.take_along_axis(step_bounds.reshape(sections, bounds_per), order, axis=1)
-    positions = jnp.transpose(ordered).reshape(-1)
-    block_of = positions // CH
-    offset = positions % CH
-    cum_b = cum[block_of]
-    cum_at = jnp.take_along_axis(cum_b, offset[:, None, None], axis=1)
-    inside_mask = lax.broadcasted_iota(jnp.int32, (1, CH), 1) <= offset[:, None]
-    bound_weight = (
-        jnp.where(inside_mask[:, :, None], jnp.exp(jnp.minimum(cum_at - cum_b, 0.0)), 0.0)
-        * step_size[block_of]
-    )
-    bound_weighted = (inner_f[block_of] * bound_weight[..., None]).astype(jnp.bfloat16)
-    inside = jnp.einsum(
-        "bshp,bsn->bhpn", bound_weighted, b_input[block_of], preferred_element_type=jnp.float32
-    )
-    states = jnp.exp(cum_at[:, 0])[..., None, None] * starts[block_of] + inside
-    states = states.astype(jnp.bfloat16).reshape(bounds_per, sections, mine, P_SIZE, N)
 
     sub = head_devices // sections
     rank = section * sub + head_block % sub

time: 812 us -> 715 us (0.88)
  waiting for transfers between devices: 415 us -> 313 us
  matrix products: 177 us -> 165 us
  local copies, waits for them, and re-layouts: 119 us -> 129 us
    all_gather x8 -> x2, waiting for transfers between devices: 324 us -> 225 us  [project(): lax.all_gather(tokens[c * rows:(c + 1) * rows], ('seq', 'heads'), axis=0)]
    dot_general x12 -> x6, matrix products: 141 us -> 135 us  [project(): lax.dot_general(part, w.reshape(head_devices, width, w.shape[1]), (((1, 3...]
  transfers between devices with their start and end apart: 13 -> 7, of which waited for: 10 -> 5; matrix products, arithmetic and copies ran while one was open for 20% -> 7% of each run, Pallas kernels for 0% -> 0%
where the time goes in v2:
time: 715 us; the launch traced here: 702 us
  waiting for transfers between devices  313 us (44%)
  matrix products  165 us (23%)
  local copies, waits for them, and re-layouts  129 us (18%)
  other arithmetic  67.3 us (9%)
  between operations  15.2 us (2%)
  starting transfers between devices  12.8 us (2%)
    all_gather x2, waiting for transfers between devices, project(): lax.all_gather(tokens[c * rows:(c + 1) * rows], ('seq', 'heads'), axis=0)  225 us
    dot_general x6, matrix products, project(): lax.dot_general(part, w.reshape(head_devices, width, w.shape[1]), (((1, 3...  135 us
    ppermute x4, waiting for transfers between devices, shards(): pieces.append(lax.ppermute(piece, ('seq', 'heads'), pairs))  87.4 us
    another operation x3, local copies, waits for them, and re-layouts, project(): jnp.stack(parts, axis=1).reshape(-1, parts[0].shape[-1])  21.5 us
    another operation x1, local copies, waits for them, and re-layouts, shards(): xz = xz.reshape(length, mine, 2, P_SIZE)  14.5 us
  transfers between devices with their start and end apart: 7, of which 5 were waited for; matrix products, arithmetic and copies ran while one was open for 7% of the time, Pallas kernels for 0%

profile of v2, /device:TPU:6, one launch (start us, length us, event | category | flops | bytes accessed | tf_op | source)
XLA Modules:
  0.0 702.3 jit_solution(17638619271848512433)
XLA Ops:
  28.0 109.8 %all-gather.7.cloned.1.call-done = bf16[4096,2048]{1,0:T(8,128)(2,1)} async-done(((bf16[256,2048]{1,0:T(8,128)(2,1)}), bf16[4096,2048]{1,0:T(8,128)(2,1)}) %all-gather.7.cloned.1.call-update) | async-done | bytes 16777232 | tf_op jit(solution)/shard_map/all_gather | solution.py:31
  137.8 12.3 %fusion.34 = bf16[4,1,256,256]{3,2,0,1:T(8,128)(2,1)} fusion(bf16[4,2048,256,1]{2,1,0,3:T(8,128)(2,1)} %bitcast.220, bf16[4,4,256,2048]{3,2,1,0:T(8,128)(2,1)} %bitcast.208), kind=kOutput, calls=%fused_computation.70 | convolution fusion | flops 4295229440 | bytes 21495808 | tf_op jit(solution)/shard_map/dot_general | solution.py:33
  150.1 115.0 %all-gather.5.cloned.1.call-done = bf16[4096,2048]{1,0:T(8,128)(2,1)} async-done(((bf16[256,2048]{1,0:T(8,128)(2,1)}), bf16[4096,2048]{1,0:T(8,128)(2,1)}) %all-gather.5.cloned.1.call-update) | async-done | bytes 16777232 | tf_op jit(solution)/shard_map/all_gather | solution.py:31
  265.1 12.4 %fusion.35 = bf16[4,1,256,256]{3,2,0,1:T(8,128)(2,1)} fusion(bf16[4,2048,256,1]{2,1,0,3:T(8,128)(2,1)} %bitcast.221, bf16[4,4,256,2048]{3,2,1,0:T(8,128)(2,1)} %bitcast.211), kind=kOutput, calls=%fused_computation.71 | convolution fusion | flops 4295229440 | bytes 21495808 | tf_op jit(solution)/shard_map/dot_general | solution.py:33
  277.4 11.0 %convolution_bitcast_fusion.2 = f32[4,1,256,16]{2,3,0,1:T(8,128)} fusion(bf16[4,4,256,2048]{3,2,1,0:T(8,128)(2,1)} %bitcast.209, bf16[2,4,8,2048]{3,2,1,0:T(8,128)(2,1)S(1)} %bitcast.222), kind=kOutput, calls=%fused_computation.72 | convolution fusion | flops 268435456 | bytes 17104896 | tf_op jit(solution)/shard_map/dot_general | solution.py:33
  288.5 10.8 %convolution_bitcast_fusion.3 = f32[4,1,256,16]{2,3,0,1:T(8,128)} fusion(bf16[4,4,256,2048]{3,2,1,0:T(8,128)(2,1)} %bitcast.212, bf16[2,4,8,2048]{3,2,1,0:T(8,128)(2,1)S(1)} %bitcast.223), kind=kOutput, calls=%fused_computation.73 | convolution fusion | flops 268435456 | bytes 17104896 | tf_op jit(solution)/shard_map/dot_general | solution.py:33
  299.3 44.5 %fusion.22 = bf16[4,1,256,2048]{3,2,0,1:T(8,128)(2,1)} fusion(bf16[4,4,256,2048]{3,2,1,0:T(8,128)(2,1)} %bitcast.213, bf16[4,2048,2048,1]{2,1,0,3:T(8,128)(2,1)} %bitcast.238), kind=kOutput, calls=%fused_computation.50 | convolution fusion | flops 34361835520 | bytes 54525952 | tf_op jit(solution)/shard_map/dot_general | solution.py:33
  343.8 44.5 %fusion.23 = bf16[4,1,256,2048]{3,2,0,1:T(8,128)(2,1)} fusion(bf16[4,4,256,2048]{3,2,1,0:T(8,128)(2,1)} %bitcast.210, bf16[4,2048,2048,1]{2,1,0,3:T(8,128)(2,1)} %bitcast.239), kind=kOutput, calls=%fused_computation.51 | convolution fusion | flops 34361835520 | bytes 54525952 | tf_op jit(solution)/shard_map/dot_general | solution.py:33
  396.1 7.5 %pad_maximum_fusion = bf16[4,2,256,2048]{3,2,0,1:T(8,128)(2,1)} fusion(bf16[4,1,256,2048]{3,2,0,1:T(8,128)(2,1)} %fusion.23, bf16[4,1,256,2048]{3,2,0,1:T(8,128)(2,1)} %fusion.22), kind=kLoop, calls=%fused_computation.28 | loop fusion | flops 4194304 | bytes 16777216 | tf_op jit(solution)/shard_map/stack | solution.py:42
  403.6 21.4 %copy.80 = bf16[4,2,256,2048]{2,1,0,3:T(2,128)(2,1)} copy(bf16[4,2,256,2048]{3,2,0,1:T(8,128)(2,1)} %pad_maximum_fusion) | data formatting | bytes 16777216 | tf_op jit(solution)/shard_map/stack | solution.py:42
  425.0 14.5 %reshape_reshape.3 = bf16[2048,16,2,64]{0,3,2,1:T(8,128)(2,1)} reshape(bf16[4,2,256,2048]{2,1,0,3:T(2,128)(2,1)} %copy.80) | data formatting | bytes 16777216 | tf_op jit(solution)/shard_map/reshape;reshape | solution.py:84
  447.6 8.4 %multiply_convert_fusion.5 = bf16[2048,1024]{0,1:T(8,128)(2,1)S(1)} fusion(f32[2051,1024]{0,1:T(8,128)S(1)} %pad_convert_fusion, f32[1024]{0:T(1024)S(1)} %bitcast.233, f32[1024]{0:T(1024)S(1)} %bitcast.231, f32[1024]{0:T(1024)S(1)} %bitcast.232, f32[1024]{0:T(1024)S(1)} %bitcast.230, f32[1024]{0:T(1024)S(1)} %dynamic-slice-done), kind=kLoop, calls=%fused_computation.40 | loop fusion | flops 27262976 | bytes 37769216 | tf_op jit(solution)/shard_map/convert_element_type | solution.py:22
  471.5 6.5 gather_fusion.1
  480.8 11.2 %gather_fusion.2 = f32[16,256,16,64]{1,3,2,0:T(8,128)} fusion(f32[8,256,16,64]{1,3,2,0:T(8,128)} %copy_convert_fusion, s32[1024]{0:T(1024)S(1)} %copy-done.18), kind=kCustom, calls=%fused_computation.2 | custom fusion | bytes 33554496 | tf_op jit(solution)/shard_map/gather | solution.py:124
  493.5 11.7 %add_convert_fusion = bf16[16,16,64,128]{3,2,1,0:T(8,128)(2,1)} fusion(f32[16,16,64,128]{3,2,1,0:T(8,128)} %gather_fusion.1, f32[16,16]{1,0:T(8,128)S(1)} %get-tuple-element.21, f32[16,256,16,64]{1,3,2,0:T(8,128)} %gather_fusion.2, f32[16,256,16]{1,2,0:T(8,128)S(1)} %select_multiply_fusion, bf16[16,256,128]{2,1,0:T(8,128)(2,1)S(1)} %gather_fusion.4), kind=kOutput, calls=%fused_computation.37 | convolution fusion | flops 1088421888 | bytes 30671872 | tf_op jit(solution)/shard_map/bshp,bsn->bhpn/dot_general | solution.py:125
  509.3 12.9 %fusion.15 = f32[8,256,16,64]{1,3,2,0:T(8,128)S(1)} fusion(f32[8,256,16,64]{1,3,2,0:T(8,128)S(1)} %fusion.30, f32[16]{0:T(128)S(1)} %copy-done.32, f32[8,256,16]{1,2,0:T(8,128)S(1)} %get-tuple-element.45, f32[8,256,256]{2,1,0:T(8,128)S(1)} %fusion.63, f32[8,16,256]{2,1,0:T(8,128)S(1)} %bitcast.202, f32[8,16,256]{2,1,0:T(8,128)S(1)} %get-tuple-element.43, ...), kind=kOutput, calls=%fused_computation.33 | convolution fusion | flops 1134559232 | bytes 23527488 | tf_op jit(solution)/shard_map/chts,cshp->cthp/dot_general | solution.py:141
  522.2 9.7 %copy.95 = f32[8,256,16,64]{1,0,3,2:T(8,128)} copy(f32[8,256,16,64]{1,3,2,0:T(8,128)S(1)} %fusion.15) | data formatting | bytes 16777216 | tf_op jit(solution)/shard_map/add | solution.py:145
  531.9 10.6 %reshape.510 = f32[4,512,1024]{1,0,2:T(4,128)} reshape(f32[8,256,16,64]{1,0,3,2:T(8,128)} %copy.95) | data formatting | bytes 16777216 | tf_op jit(solution)/shard_map/reshape | solution.py:146
  542.5 10.8 %reshape.512 = f32[4,512,1024]{1,0,2:T(4,128)} reshape(f32[2048,16,1,64]{0,3,2,1:T(8,128)} %get-tuple-element.33) | data formatting | bytes 16777216 | tf_op jit(solution)/shard_map/convert_element_type | solution.py:146
  553.3 8.3 %fusion.17 = bf16[4,512,1024]{1,0,2:T(4,128)(2,1)S(1)} fusion(f32[4,512,1024]{1,0,2:T(4,128)} %reshape.510, f32[4,512,1024]{1,0,2:T(4,128)} %reshape.512), kind=kLoop, calls=%fused_computation.41 | loop fusion | flops 12582912 | bytes 20971520 | tf_op jit(solution)/shard_map/convert_element_type | solution.py:167
  580.8 66.6 %collective-permute-done = bf16[4,16,64,128]{3,2,1,0:T(8,128)(2,1)S(1)} collective-permute-done((bf16[4,16,64,128]{3,2,1,0:T(8,128)(2,1)S(1)}, bf16[4,16,64,128]{3,2,1,0:T(8,128)(2,1)S(1)}, u32[]{:S(2)}, u32[]{:S(2)}) %collective-permute-start) | collective-permute-done | bytes 1048608 | tf_op jit(solution)/shard_map/ppermute | solution.py:158
  647.4 14.0 %collective-permute-done.2 = bf16[4,16,64,128]{3,2,1,0:T(8,128)(2,1)S(1)} collective-permute-done((bf16[4,16,64,128]{3,2,1,0:T(8,128)(2,1)S(1)}, bf16[4,16,64,128]{3,2,1,0:T(8,128)(2,1)S(1)}, u32[]{:S(2)}, u32[]{:S(2)}) %collective-permute-start.2) | collective-permute-done | bytes 1048608 | tf_op jit(solution)/shard_map/ppermute | solution.py:158
  661.4 6.8 collective-permute-done.3
  688.7 6.3 copy.98
  (167 shorter events, 99.7 us)
Async XLA Ops:
  7.2 16.4 %copy-start = (bf16[8192,64]{0,1:T(8,128)(2,1)S(1)}, bf16[8192,64]{0,1:T(8,128)(2,1)}, u32[]{:S(2)}) copy-start(bf16[8192,64]{0,1:T(8,128)(2,1)} %param.17) | copy-start | bytes 3145732
  7.2 5.1 copy-start.27
  7.2 6.3 copy-start.29
  7.2 6.9 copy-start.30
  7.2 8.7 %copy-start.31 = (f32[64]{0:T(128)S(1)}, f32[64]{0:T(128)}, u32[]{:S(2)}) copy-start(f32[64]{0:T(128)} %param.19) | copy-start | bytes 772
  7.2 130.6 %all-gather.7.cloned.1.call-start = ((), (), s32[]{:S(2)}) async-start(), calls=%async_computation.2 | async-start | bytes 17825792 | tf_op jit(solution)/shard_map/all_gather | solution.py:31
  10.5 254.6 %all-gather.5.cloned.1.call-start = ((), (), s32[]{:S(2)}) async-start(), calls=%async_computation.1 | async-start | bytes 17825792 | tf_op jit(solution)/shard_map/all_gather | solution.py:31
  343.8 44.5 %copy-start.8 = (f32[4,1,256,16]{2,3,0,1:T(8,128)S(1)}, f32[4,1,256,16]{2,3,0,1:T(8,128)}, u32[]{:S(2)}) copy-start(f32[4,1,256,16]{2,3,0,1:T(8,128)} %convolution_bitcast_fusion.2) | copy-start | bytes 196612
  343.8 44.5 %copy-start.9 = (f32[4,1,256,16]{2,3,0,1:T(8,128)S(1)}, f32[4,1,256,16]{2,3,0,1:T(8,128)}, u32[]{:S(2)}) copy-start(f32[4,1,256,16]{2,3,0,1:T(8,128)} %convolution_bitcast_fusion.3) | copy-start | bytes 196612
  343.8 44.5 %copy-start.24 = (f32[16]{0:T(128)S(1)}, f32[16]{0:T(128)}, u32[]{:S(2)}) copy-start(f32[16]{0:T(128)} %dynamic_slice.44) | copy-start | bytes 196
  343.8 44.5 %copy-start.25 = (f32[16]{0:T(128)S(1)}, f32[16]{0:T(128)}, u32[]{:S(2)}) copy-start(f32[16]{0:T(128)} %exponential_negate_fusion) | copy-start | bytes 196
  343.8 50.6 %copy-start.6 = (bf16[4,1,256,256]{3,2,0,1:T(8,128)(2,1)S(1)}, bf16[4,1,256,256]{3,2,0,1:T(8,128)(2,1)}, u32[]{:S(2)}) copy-start(bf16[4,1,256,256]{3,2,0,1:T(8,128)(2,1)} %fusion.34) | copy-start | bytes 1572868
  343.8 50.6 %copy-start.7 = (bf16[4,1,256,256]{3,2,0,1:T(8,128)(2,1)S(1)}, bf16[4,1,256,256]{3,2,0,1:T(8,128)(2,1)}, u32[]{:S(2)}) copy-start(bf16[4,1,256,256]{3,2,0,1:T(8,128)(2,1)} %fusion.35) | copy-start | bytes 1572868
  457.6 6.1 copy-start.2
  480.7 11.2 %copy-start.10 = (s32[16]{0:T(128)S(1)}, s32[16]{0:T(128)}, u32[]{:S(2)}) copy-start(s32[16]{0:T(128)} %get-tuple-element.56) | copy-start | bytes 196
  480.7 12.5 %copy-start.28 = (pred[16]{0:T(512)(128)(4,1)S(1)}, pred[16]{0:T(512)(128)(4,1)}, u32[]{:S(2)}) copy-start(pred[16]{0:T(512)(128)(4,1)} %get-tuple-element.23) | copy-start | bytes 52
  480.8 12.6 %copy-start.17 = (pred[16,256]{1,0:T(8,128)(4,1)S(1)}, pred[16,256]{1,0:T(8,128)(4,1)}, u32[]{:S(2)}) copy-start(pred[16,256]{1,0:T(8,128)(4,1)} %iota_compare_fusion.1) | copy-start | bytes 12292
  493.5 11.7 %copy-start.5 = (bf16[2048,256]{1,0:T(8,128)(2,1)S(1)}, bf16[2048,256]{1,0:T(8,128)(2,1)}, u32[]{:S(2)}) copy-start(bf16[2048,256]{1,0:T(8,128)(2,1)} %copy-done.4) | copy-start | bytes 3145732
  564.5 116.9 %all-to-all-start = ((bf16[4,512,1024]{1,2,0:T(8,128)(2,1)}), bf16[4,512,1024]{1,2,0:T(8,128)(2,1)}, u32[]{:S(2)}, u32[]{:S(2)}) async-start(bf16[4,512,1024]{1,2,0:T(8,128)(2,1)} %copy.96), calls=%async_computation | async-start | bytes 8388608 | tf_op jit(solution)/shard_map/all_to_all | solution.py:168
  574.3 73.1 %collective-permute-start = (bf16[4,16,64,128]{3,2,1,0:T(8,128)(2,1)S(1)}, bf16[4,16,64,128]{3,2,1,0:T(8,128)(2,1)S(1)}, u32[]{:S(2)}, u32[]{:S(2)}) collective-permute-start(bf16[4,16,64,128]{3,2,1,0:T(8,128)(2,1)S(1)} %get-tuple-element.35), channel_id=1, source_target_pairs={{0,0},{1,4},{2,8},{3,12},{4,1},{5,5},{6,9},{7,13},{8,2},{9,6},{10,... | collective-permute-start | bytes 3145736 | tf_op jit(solution)/shard_map/ppermute | solution.py:158
  577.2 70.2 %collective-permute-start.1 = (bf16[4,16,64,128]{3,2,1,0:T(8,128)(2,1)S(1)}, bf16[4,16,64,128]{3,2,1,0:T(8,128)(2,1)S(1)}, u32[]{:S(2)}, u32[]{:S(2)}) collective-permute-start(bf16[4,16,64,128]{3,2,1,0:T(8,128)(2,1)S(1)} %get-tuple-element.38), channel_id=1, source_target_pairs={{0,1},{1,5},{2,9},{3,13},{4,2},{5,6},{6,10},{7,14},{8,3},{9,7},{10... | collective-permute-start | bytes 3145736 | tf_op jit(solution)/shard_map/ppermute | solution.py:158
  580.7 80.7 %collective-permute-start.2 = (bf16[4,16,64,128]{3,2,1,0:T(8,128)(2,1)S(1)}, bf16[4,16,64,128]{3,2,1,0:T(8,128)(2,1)S(1)}, u32[]{:S(2)}, u32[]{:S(2)}) collective-permute-start(bf16[4,16,64,128]{3,2,1,0:T(8,128)(2,1)S(1)} %get-tuple-element.37), channel_id=1, source_target_pairs={{0,2},{1,6},{2,10},{3,14},{4,3},{5,7},{6,11},{7,15},{8,0},{9,4},{1... | collective-permute-start | bytes 3145736 | tf_op jit(solution)/shard_map/ppermute | solution.py:158
  580.7 87.5 %collective-permute-start.3 = (bf16[4,16,64,128]{3,2,1,0:T(8,128)(2,1)S(1)}, bf16[4,16,64,128]{3,2,1,0:T(8,128)(2,1)S(1)}, u32[]{:S(2)}, u32[]{:S(2)}) collective-permute-start(bf16[4,16,64,128]{3,2,1,0:T(8,128)(2,1)S(1)} %get-tuple-element.36), channel_id=1, source_target_pairs={{0,3},{1,7},{2,11},{3,15},{4,0},{5,4},{6,8},{7,12},{8,1},{9,5},{10... | collective-permute-start | bytes 3145736 | tf_op jit(solution)/shard_map/ppermute | solution.py:158
  684.5 10.5 %copy-start.1 = (bf16[8192,64]{0,1:T(8,128)(2,1)S(1)}, bf16[8192,64]{0,1:T(8,128)(2,1)}, u32[]{:S(2)}) copy-start(bf16[8192,64]{0,1:T(8,128)(2,1)} %param.17) | copy-start | bytes 3145732
  (17 other events, 42.3 us)
Sparse Core Ops, SparseCore 0:
  10.6 127.1 all-gather.6
  140.0 125.0 all-gather.4

commit v3 on v2

--- a/solution.py
+++ b/solution.py
@@ -22,13 +22,19 @@
     return jax.nn.silu(summed).astype(jnp.bfloat16)
 
 
-def project(tokens, xz_weight, bc_weight, step_weight, chunks):
+def project(tokens, xz_weight, small_weight, chunks):
     sections, head_devices = lax.axis_size("seq"), lax.axis_size("heads")
     rows = tokens.shape[0] // chunks
     width = tokens.shape[1]
-    xz, bc, step = [], [], []
+    features = xz_weight.shape[1] // 2
+    paired = xz_weight.reshape(-1, features // P_SIZE, 2, P_SIZE)
+    weight = jnp.concatenate(
+        [paired[:, :, 0].reshape(-1, features), paired[:, :, 1].reshape(-1, features)], axis=1
+    )
+    pieces = [tokens[c * rows : (c + 1) * rows] for c in range(chunks)]
+    xz, small = [], []
     for c in range(chunks):
-        part = lax.all_gather(tokens[c * rows : (c + 1) * rows], ("seq", "heads"), axis=0)
+        part = lax.all_gather(pieces[c], ("seq", "heads"), axis=0)
         part = part.reshape(sections, head_devices, rows, width)
         dot = lambda w: lax.dot_general(
             part,
@@ -36,11 +42,14 @@
             (((1, 3), (0, 1)), ((), ())),
             preferred_element_type=jnp.float32,
         )
-        xz.append(dot(xz_weight).astype(jnp.bfloat16))
-        bc.append(dot(bc_weight).astype(jnp.bfloat16))
-        step.append(dot(step_weight))
-    whole = lambda parts: jnp.stack(parts, axis=1).reshape(-1, parts[0].shape[-1])
-    return whole(xz), whole(bc), whole(step)
+        xz.append(dot(weight).astype(jnp.bfloat16))
+        small.append(dot(small_weight))
+        if c + 2 < chunks:
+            pieces[c + 2], xz[c], small[c] = lax.optimization_barrier(
+                (pieces[c + 2], xz[c], small[c])
+            )
+    whole = lambda parts: jnp.concatenate(parts, axis=1).reshape(-1, parts[0].shape[-1])
+    return whole([p[..., :features] for p in xz]), whole([p[..., features:] for p in xz]), whole(small)
 
 
 def shards(
@@ -73,17 +82,16 @@
     if whole_group:
         first_col = group * 2 * N - head_block * width_bc
         bc_weight = lax.dynamic_slice_in_dim(bc_weight, first_col, 2 * N, 1)
-    xz, bc_raw, step_raw = project(
-        tokens, xz_weight, bc_weight, own(step_weight, 1, 1), 2
-    )
+    bc_width = bc_weight.shape[1]
+    small_weight = jnp.concatenate([bc_weight, own(step_weight, 1, 1)], axis=1)
+    inner_raw, gate_raw, small = project(tokens, xz_weight, small_weight, 4)
+    bc_raw = small[:, :bc_width].astype(jnp.bfloat16)
+    step_raw = small[:, bc_width:]
     if not whole_group:
         bc_raw = lax.all_gather(bc_raw, "heads", axis=1, tiled=True)
         bc_raw = lax.dynamic_slice_in_dim(bc_raw, group * 2 * N, 2 * N, 1)
-    length = xz.shape[0]
+    length = inner_raw.shape[0]
     blocks = length // CH
-    xz = xz.reshape(length, mine, 2, P_SIZE)
-    inner_raw = xz[:, :, 0].reshape(length, mine * P_SIZE)
-    gate_raw = xz[:, :, 1]
     inner = conv_rows(inner_raw, own(conv_weight, P_SIZE, 1), own(conv_bias, P_SIZE, 0)).reshape(
         blocks, CH, mine, P_SIZE
     )
@@ -143,7 +151,7 @@
         "ctn,chpn->cthp", c_input, starts.astype(jnp.bfloat16), preferred_element_type=jnp.float32
     )
     ssd = intra + outer + own(skip_gain, 1, 0)[:, None] * inner_f
-    gated = ssd.reshape(length, mine, P_SIZE) * jax.nn.silu(gate_raw.astype(jnp.float32))
+    gated = ssd.reshape(length, mine * P_SIZE) * jax.nn.silu(gate_raw.astype(jnp.float32))
 
     sub = head_devices // sections
     rank = section * sub + head_block % sub
@@ -164,12 +172,14 @@
         1, sections, sub * sections * mine, P_SIZE, N
     )
 
-    gated = gated.astype(jnp.bfloat16).reshape(length, mine * P_SIZE)
+    gated = gated.astype(jnp.bfloat16)
     gated = lax.all_to_all(gated, "seq", split_axis=0, concat_axis=1, tiled=True)
     gated = gated.astype(jnp.float32)
     row_count = gated.shape[0]
     local_groups = max(1, block_heads // PER_GROUP)
-    square = jnp.sum(jnp.square(gated.reshape(row_count, local_groups, -1)), axis=2)
+    span = gated.shape[1] // local_groups
+    columns = [gated[:, g * span : (g + 1) * span] for g in range(local_groups)]
+    square = jnp.stack([jnp.sum(jnp.square(part), axis=1) for part in columns], axis=1)
     if block_heads < PER_GROUP:
         first_group = head_block * block_heads // PER_GROUP
         placed = lax.dynamic_update_slice_in_dim(
@@ -177,8 +187,8 @@
         )
         square = lax.dynamic_slice_in_dim(lax.psum(placed, "heads"), first_group, 1, 1)
     scale = lax.rsqrt(square / (PER_GROUP * P_SIZE) + EPSILON)
-    normed = gated.reshape(row_count, local_groups, -1) * scale[:, :, None]
-    mixed = normed.reshape(row_count, -1) * norm_gain[None]
+    normed = [part * scale[:, g : g + 1] for g, part in enumerate(columns)]
+    mixed = jnp.concatenate(normed, axis=1) * norm_gain[None]
     return (mixed.astype(jnp.bfloat16), handoff)
 
 

time: 715 us -> 723 us (1.011)
  waiting for transfers between devices: 313 us -> 153 us
  local copies, waits for them, and re-layouts: 129 us -> 283 us
  other arithmetic: 67.3 us -> 78.8 us
    all_gather x2 -> x4, waiting for transfers between devices: 225 us -> 63.8 us  [project(): part = lax.all_gather(pieces[c], ('seq', 'heads'), axis=0)]
    concatenate x0 -> x5, local copies, waits for them, and re-layouts: none -> 99.7 us  [the longest x4 93.4 us: project(): jnp.concatenate([paired[:, :, 0].reshape(-1, features), paired[:, :, 1].r...]
    unnamed x70 -> x64, local copies, waits for them, and re-layouts: 8.8 us -> 53.3 us
    slice x3 -> x10, local copies, waits for them, and re-layouts: 3.43 us -> 40.5 us  [the longest x1 23.2 us: project(): paired[:, :, 0].reshape(-1, features)]
    another operation x7 -> x3, local copies, waits for them, and re-layouts: 36 us -> 0.05 us  [the longest x3 21.5 us: project(): jnp.stack(parts, axis=1).reshape(-1, parts[0].shape[-1])]
    reshape x1 -> x5, local copies, waits for them, and re-layouts: 10.6 us -> 33.1 us  [the longest x2 22.1 us: shards(): conv_rows(inner_raw, own(conv_weight, P_SIZE, 1), own(conv_bias, P_SIZE, 0))]
    convert_element_type x2 -> x1, local copies, waits for them, and re-layouts: 13.6 us -> 0.52 us  [conv_rows(): return jax.nn.silu(summed).astype(jnp.bfloat16)]
    another operation x6 -> x4, other arithmetic: 12.7 us -> 4.79 us  [the longest x3 7.58 us: project(): jnp.stack(parts, axis=1).reshape(-1, parts[0].shape[-1])]
  transfers between devices with their start and end apart: 7 -> 9, of which waited for: 5 -> 5; matrix products, arithmetic and copies ran while one was open for 7% -> 43% of each run, Pallas kernels for 0% -> 0%
where the time goes in v3:
time: 723 us; the launch traced here: 711 us
  local copies, waits for them, and re-layouts  283 us (39%)
  matrix products  169 us (23%)
  waiting for transfers between devices  153 us (21%)
  other arithmetic  78.8 us (11%)
  between operations  14.8 us (2%)
  starting transfers between devices  12.5 us (2%)
    dot_general x8, matrix products, project(): lax.dot_general(part, w.reshape(head_devices, width, w.shape[1]), (((1, 3...  141 us
    concatenate x4, local copies, waits for them, and re-layouts, project(): jnp.concatenate([paired[:, :, 0].reshape(-1, features), paired[:, :, 1].r...  93.4 us
    ppermute x4, waiting for transfers between devices, shards(): pieces.append(lax.ppermute(piece, ('seq', 'heads'), pairs))  88.7 us
    all_gather x4, waiting for transfers between devices, project(): part = lax.all_gather(pieces[c], ('seq', 'heads'), axis=0)  63.8 us
    unnamed x64, local copies, waits for them, and re-layouts  53.3 us
    slice x1, local copies, waits for them, and re-layouts, project(): paired[:, :, 0].reshape(-1, features)  23.2 us
    reshape x2, local copies, waits for them, and re-layouts, shards(): conv_rows(inner_raw, own(conv_weight, P_SIZE, 1), own(conv_bias, P_SIZE, 0))  22.1 us
  transfers between devices with their start and end apart: 9, of which 5 were waited for; matrix products, arithmetic and copies ran while one was open for 43% of the time, Pallas kernels for 0%

profile of v3, /device:TPU:6, one launch (start us, length us, event | category | flops | bytes accessed | tf_op | source)
XLA Modules:
  0.0 711.3 jit_solution(13790283028805355455)
XLA Ops:
  11.0 41.0 %copy.67 = bf16[8192,2048]{0,1:T(8,128)(2,1)} copy(bf16[8192,2048]{1,0:T(8,128)(2,1)} %param.15) | data formatting | bytes 67108864 | tf_op args[1]
  52.1 23.2 %fusion.63 = (bf16[8192,16,1,64]{0,3,2,1:T(8,128)(2,1)}, bf16[8192,16,1,64]{0,3,2,1:T(8,128)(2,1)}) fusion(bf16[8192,16,2,64]{0,3,2,1:T(8,128)(2,1)} %bitcast.192), kind=kLoop, calls=%fused_computation.182 | loop fusion | bytes 67108864 | tf_op jit(solution)/shard_map/slice | solution.py:32
  75.2 27.9 %concatenate.24 = bf16[4,2048,1024]{1,0,2:T(4,128)(2,1)} reshape(bf16[8192,16,1,64]{0,3,2,1:T(8,128)(2,1)} %get-tuple-element.38) | data formatting | bytes 33554432 | tf_op jit(solution)/shard_map/concatenate | solution.py:31
  103.1 18.6 %copy.69 = bf16[4,2048,1024]{1,2,0:T(8,128)(2,1)} copy(bf16[4,2048,1024]{1,0,2:T(4,128)(2,1)} %concatenate.24) | data formatting | bytes 33554432 | tf_op jit(solution)/shard_map/concatenate | solution.py:31
  121.8 28.1 %concatenate.23 = bf16[4,2048,1024]{1,0,2:T(4,128)(2,1)} reshape(bf16[8192,16,1,64]{0,3,2,1:T(8,128)(2,1)} %get-tuple-element.37) | data formatting | bytes 33554432 | tf_op jit(solution)/shard_map/concatenate | solution.py:31
  149.9 18.7 %copy.68 = bf16[4,2048,1024]{1,2,0:T(8,128)(2,1)} copy(bf16[4,2048,1024]{1,0,2:T(4,128)(2,1)} %concatenate.23) | data formatting | bytes 33554432 | tf_op jit(solution)/shard_map/concatenate | solution.py:31
  176.1 9.5 %convolution_bitcast_fusion.1 = f32[4,128,272]{1,2,0:T(8,128)} fusion(bf16[4,2048,272,1]{2,1,0,3:T(8,128)(2,1)} %bitcast.200, bf16[4,4,128,2048]{3,2,1,0:T(8,128)(2,1)} %bitcast.233), kind=kOutput, calls=%fused_computation.75 | convolution fusion | flops 2281701376 | bytes 13402112 | tf_op jit(solution)/shard_map/dot_general | solution.py:39
  185.6 25.9 %fusion.24 = bf16[4,128,2048]{1,2,0:T(8,128)(2,1)} fusion(bf16[4,4,128,2048]{3,2,1,0:T(8,128)(2,1)} %bitcast.234, bf16[4,2048,1024]{1,2,0:T(8,128)(2,1)} %copy.69, bf16[4,2048,1024]{1,2,0:T(8,128)(2,1)} %copy.68), kind=kOutput, calls=%fused_computation.57 | convolution fusion | flops 17248026624 | bytes 44040192 | tf_op jit(solution)/shard_map/dot_general | solution.py:39
  211.6 9.5 %convolution_bitcast_fusion = f32[4,128,272]{1,2,0:T(8,128)} fusion(bf16[4,2048,272,1]{2,1,0,3:T(8,128)(2,1)} %bitcast.201, bf16[4,4,128,2048]{3,2,1,0:T(8,128)(2,1)} %bitcast.231), kind=kOutput, calls=%fused_computation.74 | convolution fusion | flops 2281701376 | bytes 13402112 | tf_op jit(solution)/shard_map/dot_general | solution.py:39
  221.2 26.1 %fusion.25 = bf16[4,128,2048]{1,2,0:T(8,128)(2,1)} fusion(bf16[4,4,128,2048]{3,2,1,0:T(8,128)(2,1)} %bitcast.232, bf16[4,2048,1024]{1,2,0:T(8,128)(2,1)} %copy.69, bf16[4,2048,1024]{1,2,0:T(8,128)(2,1)} %copy.68), kind=kOutput, calls=%fused_computation.58 | convolution fusion | flops 17248026624 | bytes 44040192 | tf_op jit(solution)/shard_map/dot_general | solution.py:39
  263.8 23.4 %all-gather.13.cloned.1.call-done = bf16[2048,2048]{1,0:T(8,128)(2,1)} async-done(((bf16[128,2048]{1,0:T(8,128)(2,1)}), bf16[2048,2048]{1,0:T(8,128)(2,1)}) %all-gather.13.cloned.1.call-update) | async-done | bytes 8388624 | tf_op jit(solution)/shard_map/all_gather | solution.py:37
  295.6 26.4 %bitcast_convert_fusion.1 = bf16[4,128,2048]{1,2,0:T(8,128)(2,1)} fusion(bf16[4,4,128,2048]{3,2,1,0:T(8,128)(2,1)} %bitcast.228, bf16[4,2048,1024]{1,2,0:T(8,128)(2,1)} %copy.69, bf16[4,2048,1024]{1,2,0:T(8,128)(2,1)} %copy.68), kind=kOutput, calls=%fused_computation.50 | convolution fusion | flops 17248026624 | bytes 44040192 | tf_op jit(solution)/shard_map/dot_general | solution.py:39
  322.0 40.4 %all-gather.15.cloned.1.call-done = bf16[2048,2048]{1,0:T(8,128)(2,1)} async-done(((bf16[128,2048]{1,0:T(8,128)(2,1)}), bf16[2048,2048]{1,0:T(8,128)(2,1)}) %all-gather.15.cloned.1.call-update) | async-done | bytes 8388624 | tf_op jit(solution)/shard_map/all_gather | solution.py:37
  371.3 26.2 %bitcast_convert_fusion = bf16[4,128,2048]{1,2,0:T(8,128)(2,1)} fusion(bf16[4,4,128,2048]{3,2,1,0:T(8,128)(2,1)} %bitcast.230, bf16[4,2048,1024]{1,2,0:T(8,128)(2,1)} %copy.69, bf16[4,2048,1024]{1,2,0:T(8,128)(2,1)} %copy.68), kind=kOutput, calls=%fused_computation.49 | convolution fusion | flops 17248026624 | bytes 44040192 | tf_op jit(solution)/shard_map/dot_general | solution.py:39
  428.0 11.6 %reshape.599 = bf16[8,256,16,64]{3,2,1,0:T(8,128)(2,1)} reshape(bf16[2048,1024]{1,0:T(8,128)(2,1)} %multiply_convert_fusion.5) | data formatting | bytes 8388608 | tf_op jit(solution)/shard_map/reshape | solution.py:95
  439.6 10.5 %copy.96 = bf16[8,256,16,64]{1,3,2,0:T(8,128)(2,1)} copy(bf16[8,256,16,64]{3,2,1,0:T(8,128)(2,1)} %reshape.599) | data formatting | bytes 8388608 | tf_op jit(solution)/shard_map/reshape | solution.py:95
  486.7 11.4 %gather_fusion.2 = f32[16,256,16,64]{1,3,2,0:T(8,128)} fusion(f32[8,256,16,64]{1,3,2,0:T(8,128)} %convert_element_type.81, s32[1024]{0:T(1024)S(1)} %copy-done.15), kind=kCustom, calls=%fused_computation.2 | custom fusion | bytes 33554496 | tf_op jit(solution)/shard_map/gather | solution.py:132
  501.9 12.0 %add_convert_fusion = bf16[16,16,64,128]{3,2,1,0:T(8,128)(2,1)} fusion(f32[16,16,64,128]{3,2,1,0:T(8,128)} %gather_fusion.1, f32[16,16]{1,0:T(8,128)S(1)} %get-tuple-element.27, f32[16,256,16,64]{1,3,2,0:T(8,128)} %gather_fusion.2, f32[16,256,16]{1,2,0:T(8,128)S(1)} %select_multiply_fusion, bf16[16,256,128]{2,1,0:T(8,128)(2,1)} %gather_fusion.4), kind=kOutput, calls=%fused_computation.37 | convolution fusion | flops 1088421888 | bytes 30671872 | tf_op jit(solution)/shard_map/bshp,bsn->bhpn/dot_general | solution.py:133
  516.1 11.4 %fusion.17 = f32[8,256,16,64]{1,3,2,0:T(8,128)S(1)} fusion(f32[8,256,16,64]{1,3,2,0:T(8,128)S(1)} %fusion.30, f32[16]{0:T(128)S(1)} %copy-done.28, f32[8,256,16]{1,2,0:T(8,128)S(1)} %get-tuple-element.61, bf16[8,256,16,64]{1,3,2,0:T(8,128)(2,1)S(1)} %copy-done.4, f32[8,256,256]{2,1,0:T(8,128)S(1)} %fusion.59, f32[8,16,256]{2,1,0:T(8,128)S(1)} %copy.87, ...), kind=kOutput, calls=%fused_computation.36 | convolution fusion | flops 1134559232 | bytes 23527488 | tf_op jit(solution)/shard_map/chts,cshp->cthp/dot_general | solution.py:149
  527.5 9.7 %copy.97 = f32[8,256,16,64]{1,0,3,2:T(8,128)} copy(f32[8,256,16,64]{1,3,2,0:T(8,128)S(1)} %fusion.17) | data formatting | bytes 16777216 | tf_op jit(solution)/shard_map/add | solution.py:153
  537.2 10.8 %reshape.502 = f32[4,512,1024]{1,0,2:T(4,128)} reshape(f32[8,256,16,64]{1,0,3,2:T(8,128)} %copy.97) | data formatting | bytes 16777216 | tf_op jit(solution)/shard_map/reshape | solution.py:154
  548.0 9.4 %fusion.19 = bf16[4,512,1024]{1,2,0:T(8,128)(2,1)} fusion(f32[4,512,1024]{1,0,2:T(4,128)} %reshape.502, bf16[4,128,1024]{1,2,0:T(8,128)(2,1)} %get-tuple-element.76, bf16[4,128,1024]{1,2,0:T(8,128)(2,1)S(1)} %copy-done.8, bf16[4,128,1024]{1,2,0:T(8,128)(2,1)S(1)} %copy-done.6, bf16[4,128,1024]{1,2,0:T(8,128)(2,1)S(1)} %copy-done.7), kind=kLoop, calls=%fused_computation.41 | loop fusion | flops 29360128 | bytes 16777216 | tf_op jit(solution)/shard_map/convert_element_type | solution.py:175
  573.3 41.5 %collective-permute-done.3 = bf16[4,16,64,128]{3,2,1,0:T(8,128)(2,1)S(1)} collective-permute-done((bf16[4,16,64,128]{3,2,1,0:T(8,128)(2,1)S(1)}, bf16[4,16,64,128]{3,2,1,0:T(8,128)(2,1)S(1)}, u32[]{:S(2)}, u32[]{:S(2)}) %collective-permute-start.3) | collective-permute-done | bytes 1048608 | tf_op jit(solution)/shard_map/ppermute | solution.py:166
  614.8 45.8 %collective-permute-done.2 = bf16[4,16,64,128]{3,2,1,0:T(8,128)(2,1)S(1)} collective-permute-done((bf16[4,16,64,128]{3,2,1,0:T(8,128)(2,1)S(1)}, bf16[4,16,64,128]{3,2,1,0:T(8,128)(2,1)S(1)}, u32[]{:S(2)}, u32[]{:S(2)}) %collective-permute-start.2) | collective-permute-done | bytes 1048608 | tf_op jit(solution)/shard_map/ppermute | solution.py:166
  (184 shorter events, 177.4 us)
Async XLA Ops:
  7.2 161.4 %copy-start = (bf16[8192,64]{0,1:T(8,128)(2,1)S(1)}, bf16[8192,64]{0,1:T(8,128)(2,1)}, u32[]{:S(2)}) copy-start(bf16[8192,64]{0,1:T(8,128)(2,1)} %param.17) | copy-start | bytes 3145732
  7.2 168.9 %all-gather.9.cloned.1.call-start = ((), (), s32[]{:S(2)}) async-start(), calls=%async_computation.1 | async-start | bytes 8912896 | tf_op jit(solution)/shard_map/all_gather | solution.py:37
  10.2 201.4 %all-gather.11.cloned.1.call-start = ((), (), s32[]{:S(2)}) async-start(), calls=%async_computation.2 | async-start | bytes 8912896 | tf_op jit(solution)/shard_map/all_gather | solution.py:37
  11.0 276.2 %all-gather.13.cloned.1.call-start = ((), (), s32[]{:S(2)}) async-start(), calls=%async_computation.3 | async-start | bytes 8912896 | tf_op jit(solution)/shard_map/all_gather | solution.py:37
  211.6 150.8 %all-gather.15.cloned.1.call-start = ((), (), s32[]{:S(2)}) async-start(), calls=%async_computation.4 | async-start | bytes 8912896 | tf_op jit(solution)/shard_map/all_gather | solution.py:37
  221.2 26.2 %copy-start.22 = (s32[16]{0:T(128)S(1)}, s32[16]{0:T(128)}, u32[]{:S(2)}) copy-start(s32[16]{0:T(128)} %param.26) | copy-start | bytes 196
  221.2 26.3 %copy-start.23 = (s32[16]{0:T(128)S(1)}, s32[16]{0:T(128)}, u32[]{:S(2)}) copy-start(s32[16]{0:T(128)} %param.27) | copy-start | bytes 196
  221.2 28.4 %copy-start.25 = (f32[64]{0:T(128)S(1)}, f32[64]{0:T(128)}, u32[]{:S(2)}) copy-start(f32[64]{0:T(128)} %param.18) | copy-start | bytes 772
  221.2 28.5 %copy-start.26 = (f32[64]{0:T(128)S(1)}, f32[64]{0:T(128)}, u32[]{:S(2)}) copy-start(f32[64]{0:T(128)} %param.20) | copy-start | bytes 772
  221.2 30.4 %copy-start.27 = (f32[64]{0:T(128)S(1)}, f32[64]{0:T(128)}, u32[]{:S(2)}) copy-start(f32[64]{0:T(128)} %param.19) | copy-start | bytes 772
  371.3 26.2 %copy-start.9 = (f32[4,128,272]{1,2,0:T(8,128)S(1)}, f32[4,128,272]{1,2,0:T(8,128)}, u32[]{:S(2)}) copy-start(f32[4,128,272]{1,2,0:T(8,128)} %convolution_bitcast_fusion.1) | copy-start | bytes 1671172
  371.3 26.2 %copy-start.10 = (f32[4,128,272]{1,2,0:T(8,128)S(1)}, f32[4,128,272]{1,2,0:T(8,128)}, u32[]{:S(2)}) copy-start(f32[4,128,272]{1,2,0:T(8,128)} %convolution_bitcast_fusion) | copy-start | bytes 1671172
  439.6 10.9 %copy-start.18 = (f32[1,256]{1,0:T(1,128)S(1)}, f32[1,256]{1,0:T(1,128)}, u32[]{:S(2)}) copy-start(f32[1,256]{1,0:T(1,128)} %get-tuple-element.69) | copy-start | bytes 3076
  439.6 10.9 %copy-start.19 = (f32[1,256]{1,0:T(1,128)S(1)}, f32[1,256]{1,0:T(1,128)}, u32[]{:S(2)}) copy-start(f32[1,256]{1,0:T(1,128)} %get-tuple-element.70) | copy-start | bytes 3076
  439.6 10.9 %copy-start.20 = (f32[256]{0:T(256)S(1)}, f32[256]{0:T(256)}, u32[]{:S(2)}) copy-start(f32[256]{0:T(256)} %dynamic_slice.46) | copy-start | bytes 3076
  486.7 13.7 %copy-start.11 = (s32[16]{0:T(128)S(1)}, s32[16]{0:T(128)}, u32[]{:S(2)}) copy-start(s32[16]{0:T(128)} %get-tuple-element.74) | copy-start | bytes 196
  486.7 15.0 %copy-start.24 = (pred[16]{0:T(512)(128)(4,1)S(1)}, pred[16]{0:T(512)(128)(4,1)}, u32[]{:S(2)}) copy-start(pred[16]{0:T(512)(128)(4,1)} %get-tuple-element.29) | copy-start | bytes 52
  486.7 15.1 %copy-start.14 = (pred[16,256]{1,0:T(8,128)(4,1)S(1)}, pred[16,256]{1,0:T(8,128)(4,1)}, u32[]{:S(2)}) copy-start(pred[16,256]{1,0:T(8,128)(4,1)} %iota_compare_fusion.1) | copy-start | bytes 12292
  501.9 12.0 %copy-start.2 = (f32[8,16,64,128]{3,2,1,0:T(8,128)S(1)}, f32[8,16,64,128]{3,2,1,0:T(8,128)}, u32[]{:S(2)}) copy-start(f32[8,16,64,128]{3,2,1,0:T(8,128)} %fusion.33) | copy-start | bytes 12582916
  557.4 117.7 %all-to-all-start = ((bf16[4,512,1024]{1,2,0:T(8,128)(2,1)}), bf16[4,512,1024]{1,2,0:T(8,128)(2,1)}, u32[]{:S(2)}, u32[]{:S(2)}) async-start(bf16[4,512,1024]{1,2,0:T(8,128)(2,1)} %fusion.19), calls=%async_computation | async-start | bytes 8388608 | tf_op jit(solution)/shard_map/all_to_all | solution.py:176
  567.2 47.6 %collective-permute-start.3 = (bf16[4,16,64,128]{3,2,1,0:T(8,128)(2,1)S(1)}, bf16[4,16,64,128]{3,2,1,0:T(8,128)(2,1)S(1)}, u32[]{:S(2)}, u32[]{:S(2)}) collective-permute-start(bf16[4,16,64,128]{3,2,1,0:T(8,128)(2,1)S(1)} %get-tuple-element.42), channel_id=1, source_target_pairs={{0,3},{1,7},{2,11},{3,15},{4,0},{5,4},{6,8},{7,12},{8,1},{9,5},{10... | collective-permute-start | bytes 3145736 | tf_op jit(solution)/shard_map/ppermute | solution.py:166
  567.7 92.9 %collective-permute-start.2 = (bf16[4,16,64,128]{3,2,1,0:T(8,128)(2,1)S(1)}, bf16[4,16,64,128]{3,2,1,0:T(8,128)(2,1)S(1)}, u32[]{:S(2)}, u32[]{:S(2)}) collective-permute-start(bf16[4,16,64,128]{3,2,1,0:T(8,128)(2,1)S(1)} %get-tuple-element.43), channel_id=1, source_target_pairs={{0,2},{1,6},{2,10},{3,14},{4,3},{5,7},{6,11},{7,15},{8,0},{9,4},{1... | collective-permute-start | bytes 3145736 | tf_op jit(solution)/shard_map/ppermute | solution.py:166
  568.9 91.6 %collective-permute-start.1 = (bf16[4,16,64,128]{3,2,1,0:T(8,128)(2,1)S(1)}, bf16[4,16,64,128]{3,2,1,0:T(8,128)(2,1)S(1)}, u32[]{:S(2)}, u32[]{:S(2)}) collective-permute-start(bf16[4,16,64,128]{3,2,1,0:T(8,128)(2,1)S(1)} %get-tuple-element.44), channel_id=1, source_target_pairs={{0,1},{1,5},{2,9},{3,13},{4,2},{5,6},{6,10},{7,14},{8,3},{9,7},{10... | collective-permute-start | bytes 3145736 | tf_op jit(solution)/shard_map/ppermute | solution.py:166
  571.3 90.6 %collective-permute-start = (bf16[4,16,64,128]{3,2,1,0:T(8,128)(2,1)S(1)}, bf16[4,16,64,128]{3,2,1,0:T(8,128)(2,1)S(1)}, u32[]{:S(2)}, u32[]{:S(2)}) collective-permute-start(bf16[4,16,64,128]{3,2,1,0:T(8,128)(2,1)S(1)} %get-tuple-element.41), channel_id=1, source_target_pairs={{0,0},{1,4},{2,8},{3,12},{4,1},{5,5},{6,9},{7,13},{8,2},{9,6},{10,... | collective-permute-start | bytes 3145736 | tf_op jit(solution)/shard_map/ppermute | solution.py:166
  (15 other events, 95.8 us)
Sparse Core Ops, SparseCore 0:
  10.8 75.1 all-gather.8
  88.8 73.1 all-gather.10
  211.7 75.4 all-gather.12
  289.2 73.1 all-gather.14
